TPU v7x, 128 devices: a whole 4x4x4 slice. The times are simulated.
128 devices in a mesh: prow: 8 (over x, z_lo), pcol: 16 (over y, z_hi, core).
Axes of the slice: x: 4, y: 4, z: 4 (z_hi: 2, z_lo: 2; z = z_hi * 2 + z_lo), core: 2. Of those that a mesh axis runs over, the one named last changes fastest.
Arguments:
- inverse_matrix: float32 [24576, 24576], P('prow', 'pcol'), may hold values from -6 to 6
- factor_blocks: float32 [4, 96, 256, 256], P(None, 'prow', 'pcol'), may hold values from -0.0390625 to 0.0390625
- factor_inverse: float32 [4, 256, 256], replicated, may hold values from -8 to 8, as said below
- diag_given: float32 [4, 256, 256], replicated, may hold values from -6 to 6
- block_lists: int32 [4, 96], replicated, may hold values from 0 to 95, as said below
- list_mask: int32 [4, 96], replicated, may hold values from 0 to 1, as said below
- slot_of_block: int32 [96], replicated, may hold values from 0 to 95, as said below
Outputs:
- panel_inverse: float32 [4, 96, 256, 256], P(None, 'prow', 'pcol')
- diag_inverse: float32 [4, 256, 256], replicated
Inputs may be any that keep to these rules, and one draw needn't show every extreme that they name: `block_lists`: each panel's list names every block of the window once; entries with mask 0 are padding. `list_mask`: 1 marks a used list entry; for every k, of the 48 pairs (p, s) with s // 12 = k, exactly 36 have slot_valid[p, s] = 1. `slot_of_block`: a permutation of the 96 slots. `factor_inverse`: lower triangular with a positive diagonal.
All inputs are finite; a program needn't handle non-finite values.
Results may differ from a plain program's by a relative error of at most 0.00007.
Values sent between devices are 32-bit elements; how exact they have to be, the bound alone decides.
A program may use at most 128 MiB of HBM per device.

v0:
```python
import jax
import jax.numpy as jnp
from jax import lax
from jax.sharding import Mesh
from jax.sharding import PartitionSpec as P

PROW = ("prow_0", "prow_1")
PROW_PCOL = ("prow_0", "prow_1", "pcol")


def whole_of(array, axes, dim):
    for axis in reversed(axes):
        array = lax.all_gather(array, axis, axis=dim, tiled=True)
    return array


def split_up(array, dim, length):
    before, after = (array.shape[:dim], array.shape[dim + 1 :])
    return jnp.moveaxis(array.reshape(*before, length, -1, *after), dim, 0)


def edges_of(length, count):
    hop = length // count
    if hop >= 8:
        hop -= hop % 8
    return [hop * k for k in range(1, count)]


def in_order(blocks, dim):
    dims = list(blocks.shape[1:])
    dims[dim] *= blocks.shape[0]
    return jnp.moveaxis(blocks, 0, dim).reshape(dims)


def cut_exchange(array, axis, pieces, split_dim, concat_dim):
    blocks = split_up(array, split_dim, lax.axis_size(axis))
    split_at = max(range(1, max(2, blocks.ndim - 1)), key=lambda d: blocks.shape[d])
    gathered = []
    for share in jnp.split(blocks, edges_of(blocks.shape[split_at], pieces), axis=split_at):
        if share.size:
            gathered.append(lax.all_to_all(share, axis, split_axis=0, concat_axis=0, tiled=True))
    return in_order(jnp.concatenate(gathered, axis=split_at), concat_dim)


def valid_slots(block_lists, list_mask, slot_of_block):
    window_blocks = block_lists.shape[1]
    block_ids = jnp.arange(window_blocks, dtype=jnp.int32)
    chosen = (block_lists[:, :, None] == block_ids[None, None, :]).astype(jnp.int32)
    slot_ids = jnp.sum(chosen * slot_of_block[None, None, :], axis=2)
    matches = (slot_ids[:, :, None] == block_ids[None, None, :]).astype(jnp.int32) * list_mask[
        :, :, None
    ]
    return jnp.sum(matches, axis=1)


def on_device(
    inverse_matrix, factor_blocks, factor_inverse, diag_given, block_lists, list_mask, slot_of_block
):
    highest = lax.Precision.HIGHEST
    panels = factor_blocks.shape[0]
    rows_here = factor_blocks.shape[1]
    panel_width = factor_inverse.shape[1]
    cols_here = inverse_matrix.shape[1] // panel_width
    row_index = lax.axis_index(PROW)
    slot_valid = valid_slots(block_lists, list_mask, slot_of_block).astype(jnp.float32)
    row_valid = lax.dynamic_slice_in_dim(slot_valid, row_index * rows_here, rows_here, 1)
    normalized = jnp.einsum("psij,pjk->psik", factor_blocks, factor_inverse, precision=highest)
    normalized = normalized * row_valid[:, :, None, None]
    pieces = whole_of(normalized, PROW, 1)
    column_hat = cut_exchange(pieces, "pcol", 2, 1, 2)
    stacked = column_hat.reshape(panels, cols_here * panel_width, panel_width)
    partial_value = jnp.einsum(
        "ij,pjk->pik",
        inverse_matrix,
        stacked,
        precision=highest,
        preferred_element_type=jnp.float32,
    )
    partial_value = partial_value.reshape(panels, rows_here, panel_width, panel_width)
    summed = lax.psum_scatter(partial_value, "pcol", scatter_dimension=2, tiled=True)
    panel_inverse = -(summed * row_valid[:, :, None, None])
    local_diag = jnp.einsum("psik,psil->pkl", normalized, panel_inverse, precision=highest)
    diag_inverse = diag_given - lax.psum(local_diag, PROW_PCOL)
    return (panel_inverse, diag_inverse)


def solution(mesh):
    torus = Mesh(mesh.devices.reshape(4, 2, mesh.shape["pcol"]), ("prow_0", "prow_1", "pcol"))
    return jax.shard_map(
        on_device,
        mesh=torus,
        in_specs=(P(PROW, "pcol"), P(None, PROW, "pcol", None), P(), P(), P(), P(), P()),
        out_specs=(P(None, PROW, "pcol", None), P()),
        check_vma=False,
    )
```

profile of v0, /device:TPU:1, one launch (start us, length us, event | category | flops | bytes accessed | tf_op | source)
XLA Modules:
  0.0 627.1 jit_solution(12879346787884224473)
XLA Ops:
  7.2 0.0 copy-start
  7.2 0.0 all-gather.3.cloned.1.call-start
  7.2 1.0 select_reduce_fusion.1
  8.2 0.9 select_reduce_fusion
  9.1 0.1 constant_dynamic-slice_fusion
  9.2 0.0 copy-done
  9.2 2.9 convolution_multiply_fusion
  12.1 0.0 all-gather.3.cloned.1.call-update
  12.2 0.0 all-gather.5.cloned.1.call-start
  12.2 32.9 %all-gather.3.cloned.1.call-done = f32[4,24,16,256]{3,2,1,0:T(8,128)} async-done(((f32[4,12,16,256]{3,2,1,0:T(8,128)}), f32[4,24,16,256]{3,2,1,0:T(8,128)}) %all-gather.3.cloned.1.call-update) | async-done | bytes 1572880 | tf_op jit(solution)/shard_map/all_gather | solution.py:13
  45.1 0.0 all-gather.5.cloned.1.call-update
  45.2 0.0 reduce-scatter.2.cloned.1.call-start
  45.2 68.2 %all-gather.5.cloned.1.call-done = f32[4,96,16,256]{3,2,1,0:T(8,128)} async-done(((f32[4,24,16,256]{3,2,1,0:T(8,128)}), f32[4,96,16,256]{3,2,1,0:T(8,128)}) %all-gather.5.cloned.1.call-update) | async-done | bytes 6291472 | tf_op jit(solution)/shard_map/all_gather | solution.py:13
  113.4 3.5 copy.29
  117.0 1.0 fusion.6
  117.9 46.8 %all_to_all.10 = f32[16,4,6,8,256]{4,3,2,1,0:T(8,128)S(1)} all-to-all(f32[16,4,6,8,256]{4,3,2,1,0:T(8,128)S(1)} %get-tuple-element.2), channel_id=1, replica_groups=mesh['prow_0'=4,'prow_1'=2,'pcol'=16] {'pcol'}, dimensions={0} | all-to-all | bytes 6291456 | tf_op jit(solution)/shard_map/all_to_all | solution.py:41
  164.7 43.0 %all_to_all.11 = f32[16,4,6,8,256]{4,3,2,1,0:T(8,128)S(1)} all-to-all(f32[16,4,6,8,256]{4,3,2,1,0:T(8,128)S(1)} %get-tuple-element.3), channel_id=1, replica_groups=mesh['prow_0'=4,'prow_1'=2,'pcol'=16] {'pcol'}, dimensions={0} | all-to-all | bytes 6291456 | tf_op jit(solution)/shard_map/all_to_all | solution.py:41
  207.8 0.4 pad_maximum_fusion
  208.2 1.0 copy.27
  209.3 125.3 %fusion.2 = f32[4,3072,256]{1,2,0:T(8,128)} fusion(f32[4,1536,256]{2,1,0:T(8,128)S(1)} %bitcast.29, f32[3072,1536]{1,0:T(8,128)} %param.7), kind=kOutput, calls=%fused_computation.2 | convolution fusion | flops 57982058496 | bytes 37748736 | tf_op jit(solution)/shard_map/ij,pjk->pik/dot_general | solution.py:72
  334.5 12.6 %copy.23 = f32[4,3072,256]{2,1,0:T(8,128)} copy(f32[4,3072,256]{1,2,0:T(8,128)} %fusion.2) | data formatting | bytes 25165824 | tf_op jit(solution)/shard_map/ij,pjk->pik/transpose | solution.py:72
  347.1 0.0 copy-start.2
  347.1 0.0 reduce-scatter.2.cloned.1.call-update
  347.1 0.0 copy-start.3
  347.2 0.0 copy-start.1
  347.2 0.0 all-reduce.2.cloned.1.call-start
  347.2 118.1 %reduce-scatter.2.cloned.1.call-done = f32[4,12,16,256]{3,2,1,0:T(8,128)} async-done(((f32[4,12,256,256]{3,2,1,0:T(8,128)}), f32[4,12,16,256]{3,2,1,0:T(8,128)}) %reduce-scatter.2.cloned.1.call-update) | async-done | bytes 786448 | tf_op jit(solution)/shard_map/reduce_scatter | solution.py:80
  465.3 1.2 multiply_negate_fusion
  466.5 0.0 copy-start.4
  466.6 0.9 copy-done.4
  467.4 0.0 copy-done.2
  467.4 2.8 convolution_bitcast_fusion
  470.3 0.0 all-reduce.2.cloned.1.call-update
  470.3 147.9 %all-reduce.2.cloned.1.call-done = f32[4,256,256]{2,1,0:T(8,128)} async-done(((f32[4,256,256]{2,1,0:T(8,128)}), f32[4,256,256]{2,1,0:T(8,128)}) %all-reduce.2.cloned.1.call-update) | async-done | bytes 1048592 | tf_op jit(solution)/shard_map/psum | solution.py:83
  618.3 0.0 copy-done.3
  618.3 2.3 sub.3
  620.6 0.0 copy-done.1
  (1 shorter events, 0.0 us)
Async XLA Ops:
  7.2 2.0 copy-start
  7.2 38.0 %all-gather.3.cloned.1.call-start = ((), (), s32[]{:S(2)}) async-start(), calls=%async_computation.3 | async-start | bytes 2359296 | tf_op jit(solution)/shard_map/all_gather | solution.py:13
  12.2 101.2 %all-gather.5.cloned.1.call-start = ((), (), s32[]{:S(2)}) async-start(), calls=%async_computation.4 | async-start | bytes 7864320 | tf_op jit(solution)/shard_map/all_gather | solution.py:13
  45.2 420.1 %reduce-scatter.2.cloned.1.call-start = ((), (), s32[]{:S(2)}) async-start(), calls=%async_computation.5 | async-start | bytes 13369344 | tf_op jit(solution)/shard_map/reduce_scatter | solution.py:80
  347.1 120.3 %copy-start.2 = (f32[4,12,16,256]{3,2,1,0:T(8,128)S(1)}, f32[4,12,16,256]{3,2,1,0:T(8,128)}, u32[]{:S(2)}) copy-start(f32[4,12,16,256]{3,2,1,0:T(8,128)} %convolution_multiply_fusion) | copy-start | bytes 2359300
  347.1 271.1 %copy-start.3 = (f32[4,256,256]{2,1,0:T(8,128)S(1)}, f32[4,256,256]{2,1,0:T(8,128)}, u32[]{:S(2)}) copy-start(f32[4,256,256]{2,1,0:T(8,128)} %param.10) | copy-start | bytes 3145732
  347.2 273.4 %copy-start.1 = (f32[4,256,256]{2,1,0:T(8,128)S(1)}, f32[4,256,256]{2,1,0:T(8,128)}, u32[]{:S(2)}) copy-start(f32[4,256,256]{2,1,0:T(8,128)} %param.9) | copy-start | bytes 3145732
  347.2 271.1 %all-reduce.2.cloned.1.call-start = ((), (), s32[]{:S(2)}) async-start(), calls=%async_computation.6 | async-start | bytes 2097152 | tf_op jit(solution)/shard_map/psum | solution.py:83
  466.5 0.9 copy-start.4
Sparse Core Ops, SparseCore 0:
  12.3 32.8 all-gather.2
  46.8 66.5 all-gather.4
  347.3 117.9 reduce-scatter.1
  470.5 147.6 all-reduce.1
where the time goes:
time: 628 us; the launch traced here: 627 us
  waiting for transfers between devices  367 us (58%)
  matrix products  131 us (21%)
  blocking collectives  89.8 us (14%)
  local copies, waits for them, and re-layouts  19.1 us (3%)
  between operations  13.9 us (2%)
    psum x1, waiting for transfers between devices, on_device(): diag_inverse = diag_given - lax.psum(local_diag, PROW_PCOL)  148 us
    dot_general x1, matrix products, on_device(): jnp.einsum('ij,pjk->pik', inverse_matrix, stacked, precision=highest, pre...  125 us
    reduce_scatter x1, waiting for transfers between devices, on_device(): lax.psum_scatter(partial_value, 'pcol', scatter_dimension=2, tiled=True)  118 us
    all_gather x2, waiting for transfers between devices, whole_of(): array = lax.all_gather(array, axis, axis=dim, tiled=True)  101 us
    all_to_all x2, blocking collectives, cut_exchange(): lax.all_to_all(share, axis, split_axis=0, concat_axis=0, tiled=True)  89.8 us
    transpose x1, local copies, waits for them, and re-layouts, on_device(): jnp.einsum('ij,pjk->pik', inverse_matrix, stacked, precision=highest, pre...  12.6 us
  transfers between devices with their start and end apart: 4, of which 4 were waited for; matrix products, arithmetic and copies ran while one was open for 0% of the time, Pallas kernels for 0%

commit v1 on v0

v1 whole, which is shorter than its diff:
```python
import functools

import jax
import jax.numpy as jnp
from jax import lax
from jax.experimental import pallas as pl
from jax.experimental.pallas import tpu as pltpu
from jax.sharding import PartitionSpec as P

MESH = pl.DeviceIdType.MESH
F32 = jnp.float32
BF16 = jnp.bfloat16
KEEP = 36
HALF_A = 16
NEED = 24
QR = 3


def coords():
    k = lax.axis_index("prow")
    j = lax.axis_index("pcol")
    return k // 2, j // 4, (j // 2) % 2, k % 2, j % 2


def dev(x, y, zh, zl, c):
    return (x * 2 + zl, (y * 2 + zh) * 2 + c)


def split2(v):
    hi = v.astype(BF16)
    lo = (v - hi.astype(F32)).astype(BF16)
    return hi, lo


def dot3(ah, al, bh, bl):
    out = jnp.dot(ah, bh, preferred_element_type=F32)
    out += jnp.dot(ah, bl, preferred_element_type=F32)
    out += jnp.dot(al, bh, preferred_element_type=F32)
    return out


def valid_slots(block_lists, list_mask, slot_of_block):
    window_blocks = block_lists.shape[1]
    block_ids = jnp.arange(window_blocks, dtype=jnp.int32)
    chosen = (block_lists[:, :, None] == block_ids[None, None, :]).astype(jnp.int32)
    slot_ids = jnp.sum(chosen * slot_of_block[None, None, :], axis=2)
    matches = (slot_ids[:, :, None] == block_ids[None, None, :]).astype(jnp.int32) * list_mask[
        :, :, None
    ]
    return jnp.sum(matches, axis=1)


def packed_order(valid, group):
    v = lax.dynamic_slice_in_dim(valid, group * 12, 12, 1)
    v = v.reshape(4, 2, 6).transpose(1, 0, 2).reshape(48)
    i = jnp.arange(48, dtype=jnp.int32)
    pos = jnp.sum(v[None, :] * (i[None, :] < i[:, None]).astype(jnp.int32), axis=1)
    q = jnp.arange(KEEP, dtype=jnp.int32)
    hit = (pos[None, :] == q[:, None]).astype(jnp.int32) * v[None, :]
    idx = jnp.sum(hit * i[None, :], axis=1)
    return jnp.where(v > 0, pos, -1), idx


def prep_kernel(tab, f_ref, inv_ref, nc_ref, nd_ref):
    for p in range(4):
        nd_ref[p] = jnp.dot(
            f_ref[p].reshape(192, 256),
            inv_ref[p],
            precision=lax.Precision.HIGHEST,
            preferred_element_type=F32,
        ).reshape(12, 16, 256)

    @pl.loop(0, KEEP)
    def _(q):
        nc_ref[q] = nd_ref[tab[1, q], tab[0, q]]


def main_kernel(
    tab, g_hbm, nc, out, ghi, glo, stage, ng, nhi, nlo, pb, rc, ra, rb, rp, rm, rz,
    g_sem, p1_s, p1_r, xp_s, xp_r, xm_s, xm_r, z_s, z_r, c_s, c_r, rs_s, rs_r,
):
    x, y, zh, zl, c = coords()
    xp, xm, xf = (x + 1) % 4, (x + 3) % 4, (x + 2) % 4
    yp, ym, yf = (y + 1) % 4, (y + 3) % 4, (y + 2) % 4
    zn = 1 - zl
    d_xp, d_xm = dev(xp, y, zh, zl, c), dev(xm, y, zh, zl, c)
    d_zn, d_c = dev(x, y, zh, zn, c), dev(x, y, zh, zl, 1 - c)
    d_yp, d_ym = dev(x, yp, zh, zl, c), dev(x, ym, zh, zl, c)
    d_z2 = dev(x, y, 1 - zh, zl, c)
    d_to = dev((x + y) % 4, x, zl, zh, c)
    d_from = dev(y, (x + 4 - y) % 4, zl, zh, c)
    own_target = ((x == 0) & (y == 0)) & (zl == zh)

    barrier = pltpu.get_barrier_semaphore()
    for d in (d_xp, d_xm, d_zn, d_c, d_yp, d_ym, d_z2):
        pl.semaphore_signal(barrier, inc=1, device_id=d, device_id_type=MESH)

    @pl.when(jnp.logical_not(own_target))
    def _():
        for d in (d_to, d_from):
            pl.semaphore_signal(barrier, inc=1, device_id=d, device_id_type=MESH)
        pl.semaphore_wait(barrier, 9)

    @pl.when(own_target)
    def _():
        pl.semaphore_wait(barrier, 7)

    def share(xx, z):
        return 2 * (2 * ((xx + 4 - y) % 4) + z) + c

    r_me = (y * 2 + zh) * 2 + c
    s_o, s_l, s_r, s_f = (share(v, zl) for v in (x, xm, xp, xf))
    t_o, t_l, t_r, t_f = (share(v, zn) for v in (x, xm, xp, xf))
    a0, a1, a2 = 0, HALF_A // 2, HALF_A
    b1, b2 = (HALF_A + KEEP) // 2, KEEP

    def rcopy(src, dst, ss, rs, d):
        return pltpu.make_async_remote_copy(
            src_ref=src, dst_ref=dst, send_sem=ss, recv_sem=rs, device_id=d, device_id_type=MESH
        )

    def piece(lo, hi, s):
        return ng.at[pl.ds(lo, hi - lo), s]

    spans = ((a0, a2), (a2, b2))

    def p1(i):
        lo, hi = spans[i]
        return rcopy(nc.at[pl.ds(lo, hi - lo)], piece(lo, hi, r_me), p1_s.at[i], p1_r.at[i], d_to)

    def p1_local(i):
        lo, hi = spans[i]
        return pltpu.make_async_copy(nc.at[pl.ds(lo, hi - lo)], piece(lo, hi, s_o), p1_r.at[i])

    @pl.when(jnp.logical_not(own_target))
    def _():
        p1(0).start()
        p1(1).start()

    @pl.when(own_target)
    def _():
        p1_local(0).start()
        p1_local(1).start()

    def g_copy(i, slot):
        return pltpu.make_async_copy(
            g_hbm.at[pl.ds(i * 256, 256), :], stage.at[slot], g_sem.at[slot]
        )

    g_copy(0, 0).start()

    def load_g(i, carry):
        slot = i % 2
        g_copy(i, slot).wait()

        @pl.when(i < 11)
        def _():
            g_copy(i + 1, 1 - slot).start()

        for r in range(0, 256, 64):
            hi, lo = split2(stage[slot, r : r + 64, :])
            ghi[i, r : r + 64, :] = hi
            glo[i, r : r + 64, :] = lo
        return carry

    lax.fori_loop(0, 12, load_g, 0)

    to_xp = (
        (a0, a2, s_o), (a2, b2, s_o), (a2, b2, t_o), (a0, a1, s_l), (a2, b1, s_l), (a2, b1, t_l),
    )
    to_xm = (
        (a0, a2, s_o), (a2, b2, s_o), (a2, b2, t_o), (a1, a2, s_r), (b1, b2, s_r), (b1, b2, t_r),
    )
    to_z = ((a0, a2, s_o), (a2, b2, s_o), (a0, a2, s_l), (a0, a2, s_r), (a0, a1, s_f), (a1, a2, s_f))
    of_xm = (
        (a0, a2, s_l), (a2, b2, s_l), (a2, b2, t_l), (a0, a1, s_f), (a2, b1, s_f), (a2, b1, t_f),
    )
    of_xp = (
        (a0, a2, s_r), (a2, b2, s_r), (a2, b2, t_r), (a1, a2, s_f), (b1, b2, s_f), (b1, b2, t_f),
    )
    of_z = ((a0, a2, t_o), (a2, b2, t_o), (a0, a2, t_l), (a0, a2, t_r), (a0, a1, t_f), (a1, a2, t_f))

    def go(table, sems, d, i):
        lo, hi, s = table[i]
        return rcopy(piece(lo, hi, s), piece(lo, hi, s), sems[0].at[i], sems[1].at[i], d)

    xps, xms, zs = (xp_s, xp_r), (xm_s, xm_r), (z_s, z_r)

    def send_xp(i):
        go(to_xp, xps, d_xp, i).start()

    def send_xm(i):
        go(to_xm, xms, d_xm, i).start()

    def send_z(i):
        go(to_z, zs, d_zn, i).start()

    def got_xm(i):
        go(of_xm, xps, d_xp, i).wait_recv()

    def got_xp(i):
        go(of_xp, xms, d_xm, i).wait_recv()

    def got_z(i):
        go(of_z, zs, d_zn, i).wait_recv()

    def twin(i, s, mine):
        first = (1 - c if mine else c) * (KEEP - NEED)
        return rcopy(
            ng.at[pl.ds(first, NEED), s], ng.at[pl.ds(first, NEED), s], c_s.at[i], c_r.at[i], d_c
        )

    order = (s_o, s_l, s_r, t_o, s_f, t_l, t_r, t_f)

    def send_c(i):
        twin(i, order[i], True).start()

    @pl.when(jnp.logical_not(own_target))
    def _():
        p1(0).wait_recv()

    @pl.when(own_target)
    def _():
        p1_local(0).wait()

    send_xp(0)
    send_xm(0)
    send_z(0)

    @pl.when(jnp.logical_not(own_target))
    def _():
        p1(1).wait_recv()

    @pl.when(own_target)
    def _():
        p1_local(1).wait()

    send_xp(1)
    send_xm(1)
    send_z(1)
    send_c(0)
    got_xm(0)
    send_xp(3)
    send_z(2)
    got_xp(0)
    send_xm(3)
    send_z(3)
    got_xm(1)
    send_xp(4)
    send_c(1)
    got_xp(1)
    send_xm(4)
    send_c(2)
    got_z(0)
    got_z(1)
    send_xp(2)
    send_xm(2)
    send_c(3)
    got_xm(3)
    send_z(4)
    got_xp(3)
    send_z(5)
    got_xm(2)
    send_xp(5)
    got_xp(2)
    send_xm(5)
    got_xm(4)
    got_xp(4)
    send_c(4)
    got_z(2)
    send_c(5)
    got_z(3)
    send_c(6)
    got_xm(5)
    got_xp(5)
    got_z(4)
    got_z(5)
    send_c(7)
    for i in range(8):
        twin(i, order[i] + 1 - 2 * c, False).wait_recv()

    def spread(i, carry):
        p, t = i // 6, i % 6
        at = tab[2, i]
        used = at >= 0
        block = jnp.where(used, ng[jnp.maximum(at, 0)].reshape(256, 256), 0.0)
        hi, lo = split2(block)
        nhi[p, t] = hi
        nlo[p, t] = lo
        return carry

    lax.fori_loop(0, 24, spread, 0)

    rounds = KEEP // QR

    def product(q):
        s, p = tab[0, q], tab[1, q]
        bh = nhi[p].reshape(1536, 256)
        bl = nlo[p].reshape(1536, 256)
        pb[q] = dot3(ghi[s], glo[s], bh, bl).reshape(4, 2, 2, 16, 256)

    def m_core(g, mine):
        qs = pl.ds(g * QR, QR)
        return rcopy(pb.at[qs, :, :, 1 - c], rc.at[qs], rs_s.at[0, g], rs_r.at[0, g], d_c)

    def m_a(g):
        qs = pl.ds(g * QR, QR)
        return rcopy(pb.at[qs, yf, 0, c], ra.at[qs], rs_s.at[1, g], rs_r.at[1, g], d_yp)

    def m_b(g):
        qs = pl.ds(g * QR, QR)
        return rcopy(pb.at[qs, yf, 1, c], rb.at[qs], rs_s.at[2, g], rs_r.at[2, g], d_ym)

    def m_p(g):
        qs = pl.ds(g * QR, QR)
        return rcopy(pb.at[qs, yp, :, c], rp.at[qs], rs_s.at[3, g], rs_r.at[3, g], d_yp)

    def m_m(g):
        qs = pl.ds(g * QR, QR)
        return rcopy(pb.at[qs, ym, :, c], rm.at[qs], rs_s.at[4, g], rs_r.at[4, g], d_ym)

    def m_z(g):
        qs = pl.ds(g * QR, QR)
        return rcopy(pb.at[qs, y, 1 - zh, c], rz.at[qs], rs_s.at[5, g], rs_r.at[5, g], d_z2)

    def step(i, carry):
        @pl.when(i < rounds)
        def _():
            @pl.loop(0, QR)
            def _(n):
                product(i * QR + n)

            m_core(i, True).start()

        @pl.when((i >= 1) & (i < rounds + 1))
        def _():
            g = i - 1
            m_core(g, False).wait_recv()

            @pl.loop(0, QR)
            def _(n):
                q = g * QR + n
                pb[q, :, :, c] += rc[q]

            m_a(g).start()
            m_b(g).start()

        @pl.when((i >= 2) & (i < rounds + 2))
        def _():
            g = i - 2
            m_a(g).wait_recv()
            m_b(g).wait_recv()

            @pl.loop(0, QR)
            def _(n):
                q = g * QR + n
                pb[q, yp, 0, c] += ra[q]
                pb[q, ym, 1, c] += rb[q]

            m_p(g).start()
            m_m(g).start()

        @pl.when((i >= 3) & (i < rounds + 3))
        def _():
            g = i - 3
            m_p(g).wait_recv()
            m_m(g).wait_recv()

            @pl.loop(0, QR)
            def _(n):
                q = g * QR + n
                pb[q, y, :, c] += rp[q] + rm[q]

            m_z(g).start()

        @pl.when(i >= 4)
        def _():
            g = i - 4
            m_z(g).wait_recv()

            @pl.loop(0, QR)
            def _(n):
                q = g * QR + n
                out[q] = -(pb[q, y, zh, c] + rz[q])

        return carry

    lax.fori_loop(0, rounds + 4, step, 0)

    @pl.when(jnp.logical_not(own_target))
    def _():
        p1(0).wait_send()
        p1(1).wait_send()

    for i in range(6):
        go(to_xp, xps, d_xp, i).wait_send()
        go(to_xm, xms, d_xm, i).wait_send()
        go(to_z, zs, d_zn, i).wait_send()
    for i in range(8):
        twin(i, order[i], True).wait_send()

    @pl.loop(0, rounds)
    def _(g):
        m_core(g, True).wait_send()
        m_a(g).wait_send()
        m_b(g).wait_send()
        m_p(g).wait_send()
        m_m(g).wait_send()
        m_z(g).wait_send()


def tail_kernel(tab, pi_ref, nd_ref, out_ref, d_ref):
    for p in range(4):
        for s in range(12):
            at = tab[3, (s // 6) * 24 + p * 6 + s % 6]
            out_ref[p, s] = jnp.where(at >= 0, pi_ref[jnp.maximum(at, 0)], 0.0)
    for p in range(4):
        d_ref[p] = lax.dot_general(
            nd_ref[p].reshape(192, 256),
            out_ref[p].reshape(192, 256),
            (((0,), (0,)), ((), ())),
            precision=lax.Precision.HIGHEST,
            preferred_element_type=F32,
        )


def sum_kernel(d_ref, out, work, r0, r1, r2, r3, s_sem, r_sem):
    x, y, zh, zl, c = coords()
    z = 2 * zh + zl
    first = jnp.where(c == 0, x, y)
    second = jnp.where(c == 0, y, x)

    def peer(axis, step):
        if axis == 0:
            a, b, e = (first + step) % 4, second, z
        elif axis == 1:
            a, b, e = first, (second + step) % 4, z
        else:
            a, b, e = first, second, (z + step) % 4
        xx, yy = jnp.where(c == 0, a, b), jnp.where(c == 0, b, a)
        return dev(xx, yy, e // 2, e % 2, c)

    twin = dev(x, y, zh, zl, 1 - c)
    barrier = pltpu.get_barrier_semaphore()
    pl.semaphore_signal(barrier, inc=1, device_id=twin, device_id_type=MESH)
    for axis in range(3):
        for step in (1, 2, 3):
            pl.semaphore_signal(barrier, inc=1, device_id=peer(axis, step), device_id_type=MESH)
    pl.semaphore_wait(barrier, 10)

    def rcopy(src, dst, i, d):
        return pltpu.make_async_remote_copy(
            src_ref=src, dst_ref=dst, send_sem=s_sem.at[i], recv_sem=r_sem.at[i],
            device_id=d, device_id_type=MESH,
        )

    pending = []
    cp = rcopy(d_ref.at[1 - c], r0, 0, twin)
    cp.start()
    cp.wait_recv()
    pending.append(cp)
    work[...] = d_ref[c] + r0[...]
    at = (first, second, z)
    recv = (r1, r2, r3)
    n = 1
    for axis in range(3):
        view = work
        for a in range(axis):
            view = view.at[at[a]]
        cps = []
        for step in (1, 3, 2):
            cp = rcopy(view.at[(at[axis] + step) % 4], recv[axis].at[step - 1], n, peer(axis, step))
            n += 1
            cp.start()
            cps.append(cp)
        for cp in cps:
            cp.wait_recv()
        pending += cps
        mine = view.at[at[axis]]
        mine[...] = mine[...] + (recv[axis][0] + recv[axis][1] + recv[axis][2])
    me = out.at[c, at[0], at[1], at[2]]
    me[...] = work[at[0], at[1], at[2]]
    for axis in (2, 1, 0):
        part = out.at[c]
        for a in range(axis + 1):
            part = part.at[at[a]]
        cps = []
        for step in (1, 3, 2):
            cp = rcopy(part, part, n, peer(axis, step))
            n += 1
            cp.start()
            cps.append(cp)
        for cp in cps:
            cp.wait_recv()
        pending += cps
    cp = rcopy(out.at[c], out.at[c], n, twin)
    cp.start()
    cp.wait_recv()
    pending.append(cp)
    for cp in pending:
        cp.wait_send()


VM = pl.BlockSpec(memory_space=pltpu.VMEM)
SM = pl.BlockSpec(memory_space=pltpu.SMEM)
ANY = pl.BlockSpec(memory_space=pl.ANY)
DMA = pltpu.SemaphoreType.DMA


def on_device(
    inverse_matrix, factor_blocks, factor_inverse, diag_given, block_lists, list_mask, slot_of_block
):
    k = lax.axis_index("prow")
    j = lax.axis_index("pcol")
    valid = valid_slots(block_lists, list_mask, slot_of_block)
    pos_row, idx = packed_order(valid, k)
    pos_col, _ = packed_order(valid, j // 2)
    s_q = (idx // 24) * 6 + idx % 6
    p_q = (idx % 24) // 6
    col = lax.dynamic_slice_in_dim(pos_col, (j % 2) * 24, 24, 0)
    tab = jnp.stack(
        [jnp.pad(s_q, (0, 12)), jnp.pad(p_q, (0, 12)), jnp.pad(col, (0, 24)), pos_row]
    )

    nc, nd = pl.pallas_call(
        prep_kernel,
        out_shape=(
            jax.ShapeDtypeStruct((KEEP, 16, 256), F32),
            jax.ShapeDtypeStruct((4, 12, 16, 256), F32),
        ),
        in_specs=[SM, VM, VM],
        out_specs=(VM, VM),
        name="normalize",
    )(tab, factor_blocks, factor_inverse)

    rounds = KEEP // QR
    pi = pl.pallas_call(
        main_kernel,
        out_shape=jax.ShapeDtypeStruct((KEEP, 16, 256), F32),
        in_specs=[SM, ANY, VM],
        out_specs=VM,
        scratch_shapes=[
            pltpu.VMEM((12, 256, 1536), BF16),
            pltpu.VMEM((12, 256, 1536), BF16),
            pltpu.VMEM((2, 256, 1536), F32),
            pltpu.VMEM((KEEP, 16, 16, 256), F32),
            pltpu.VMEM((4, 6, 256, 256), BF16),
            pltpu.VMEM((4, 6, 256, 256), BF16),
            pltpu.VMEM((KEEP, 4, 2, 2, 16, 256), F32),
            pltpu.VMEM((KEEP, 4, 2, 16, 256), F32),
            pltpu.VMEM((KEEP, 16, 256), F32),
            pltpu.VMEM((KEEP, 16, 256), F32),
            pltpu.VMEM((KEEP, 2, 16, 256), F32),
            pltpu.VMEM((KEEP, 2, 16, 256), F32),
            pltpu.VMEM((KEEP, 16, 256), F32),
            DMA((2,)),
            DMA((2,)),
            DMA((2,)),
            DMA((6,)),
            DMA((6,)),
            DMA((6,)),
            DMA((6,)),
            DMA((6,)),
            DMA((6,)),
            DMA((8,)),
            DMA((8,)),
            DMA((6, rounds)),
            DMA((6, rounds)),
        ],
        compiler_params=pltpu.CompilerParams(
            collective_id=0, has_side_effects=True, vmem_limit_bytes=67043328
        ),
        name="window",
    )(tab, inverse_matrix, nc)

    panel_inverse, terms = pl.pallas_call(
        tail_kernel,
        out_shape=(
            jax.ShapeDtypeStruct((4, 12, 16, 256), F32),
            jax.ShapeDtypeStruct((4, 256, 256), F32),
        ),
        in_specs=[SM, VM, VM],
        out_specs=(VM, VM),
        name="unpack",
    )(tab, pi, nd)

    total = pl.pallas_call(
        sum_kernel,
        out_shape=jax.ShapeDtypeStruct((2, 4, 4, 4, 8, 256), F32),
        in_specs=[VM],
        out_specs=VM,
        scratch_shapes=[
            pltpu.VMEM((4, 4, 4, 8, 256), F32),
            pltpu.VMEM((4, 4, 4, 8, 256), F32),
            pltpu.VMEM((3, 4, 4, 8, 256), F32),
            pltpu.VMEM((3, 4, 8, 256), F32),
            pltpu.VMEM((3, 8, 256), F32),
            DMA((20,)),
            DMA((20,)),
        ],
        compiler_params=pltpu.CompilerParams(collective_id=1, has_side_effects=True),
        name="diag_sum",
    )(terms.reshape(2, 4, 4, 4, 8, 256))
    diag_inverse = diag_given - total.reshape(4, 256, 256)
    return (panel_inverse, diag_inverse)


def solution(mesh):
    return jax.shard_map(
        on_device,
        mesh=mesh,
        in_specs=(P("prow", "pcol"), P(None, "prow", "pcol", None), P(), P(), P(), P(), P()),
        out_specs=(P(None, "prow", "pcol", None), P()),
        check_vma=False,
    )
```

time: 628 us -> 171 us (0.27)
  waiting for transfers between devices: 367 us -> 0 us
  Pallas kernels: 0 us -> 163 us
  matrix products: 131 us -> 0 us
  blocking collectives: 89.8 us -> 0 us
  local copies, waits for them, and re-layouts: 19.1 us -> 0.6 us
  between operations: 13.9 us -> 0.73 us
    pallas_call x0 -> x4, Pallas kernels: none -> 163 us  [the longest x1 120 us: on_device(): pl.pallas_call(main_kernel, out_shape=jax.ShapeDtypeStruct((KEEP, 16, 256...]
    psum x1 -> x0, waiting for transfers between devices: 148 us -> none  [on_device(): diag_inverse = diag_given - lax.psum(local_diag, PROW_PCOL)]
    dot_general x3 -> x0, matrix products: 131 us -> none  [the longest x1 125 us: on_device(): jnp.einsum('ij,pjk->pik', inverse_matrix, stacked, precision=highest, pre...]
    reduce_scatter x1 -> x0, waiting for transfers between devices: 118 us -> none  [on_device(): lax.psum_scatter(partial_value, 'pcol', scatter_dimension=2, tiled=True)]
    all_gather x2 -> x0, waiting for transfers between devices: 101 us -> none  [whole_of(): array = lax.all_gather(array, axis, axis=dim, tiled=True)]
    all_to_all x2 -> x0, blocking collectives: 89.8 us -> none  [cut_exchange(): lax.all_to_all(share, axis, split_axis=0, concat_axis=0, tiled=True)]
    transpose x1, local copies, waits for them, and re-layouts: 12.6 us -> 0.01 us  [packed_order(): v = v.reshape(4, 2, 6).transpose(1, 0, 2).reshape(48)]
  transfers between devices with their start and end apart: 4 -> 0, of which waited for: 4 -> 0; matrix products, arithmetic and copies ran while one was open for 0% -> 0% of each run, Pallas kernels for 0% -> 0%
where the time goes in v1:
time: 171 us; the launch traced here: 170 us
  Pallas kernels  163 us (95%)
  other arithmetic  5.42 us (3%)
    pallas_call x1, Pallas kernels, on_device(): pl.pallas_call(main_kernel, out_shape=jax.ShapeDtypeStruct((KEEP, 16, 256...  120 us
    pallas_call x1, Pallas kernels, on_device(): pl.pallas_call(sum_kernel, out_shape=jax.ShapeDtypeStruct((2, 4, 4, 4, 8,...  36.4 us
    pallas_call x1, Pallas kernels, on_device(): pl.pallas_call(prep_kernel, out_shape=(jax.ShapeDtypeStruct((KEEP, 16, 25...  3.8 us
    pallas_call x1, Pallas kernels, on_device(): pl.pallas_call(tail_kernel, out_shape=(jax.ShapeDtypeStruct((4, 12, 16, 2...  3.45 us

profile of v1, /device:TPU:1, one launch (start us, length us, event | category | flops | bytes accessed | tf_op | source)
XLA Modules:
  0.0 170.0 jit_solution(7964825449352353230)
XLA Ops:
  0.7 0.9 select_reduce_fusion.1
  1.6 0.9 select_reduce_fusion
  2.5 0.1 constant_dynamic-slice_fusion
  2.5 0.1 reshape.47
  2.6 0.1 reshape.48
  2.7 0.1 select_reduce_fusion.2
  2.8 0.1 dynamic_slice.11
  2.9 0.1 reshape.46
  3.0 0.1 gt.18
  3.1 0.1 mul.70
  3.2 0.1 select_reduce_fusion.3
  3.3 0.1 multiply_reduce_fusion
  3.5 0.6 pad_add_fusion.tab
  4.1 3.8 %normalize.1 = (f32[36,16,256]{2,1,0:T(8,128)}, f32[4,12,16,256]{3,2,1,0:T(8,128)}) custom-call(s32[4,48]{1,0:T(4,128)} %pad_add_fusion.tab, f32[4,12,16,256]{3,2,1,0:T(8,128)} %f_ref.1, f32[4,256,256]{2,1,0:T(8,128)} %inv_ref.1), custom_call_target="tpu_custom_call" | custom-call | tf_op jit(solution)/shard_map/normalize/pallas_call | solution.py:525
  7.9 119.5 %window.1.pi_ref = f32[36,16,256]{2,1,0:T(8,128)} custom-call(s32[4,48]{1,0:T(4,128)} %pad_add_fusion.tab, f32[3072,1536]{1,0:T(8,128)} %g_hbm.1, f32[36,16,256]{2,1,0:T(8,128)} %get-tuple-element.6.nc), custom_call_target="tpu_custom_call" | custom-call | tf_op jit(solution)/shard_map/window/pallas_call | solution.py:537
  127.4 3.5 %unpack.1 = (f32[4,12,16,256]{3,2,1,0:T(8,128)}, f32[4,256,256]{2,1,0:T(8,128)}) custom-call(s32[4,48]{1,0:T(4,128)} %pad_add_fusion.tab, f32[36,16,256]{2,1,0:T(8,128)} %window.1.pi_ref, f32[4,12,16,256]{3,2,1,0:T(8,128)} %get-tuple-element.7.nd_ref), custom_call_target="tpu_custom_call" | custom-call | tf_op jit(solution)/shard_map/unpack/pallas_call | solution.py:576
  130.9 36.4 %diag_sum.1 = f32[2,4,4,4,8,256]{5,4,3,2,1,0:T(8,128)} custom-call(f32[2,4,4,4,8,256]{5,4,3,2,1,0:T(8,128)} %bitcast.17), custom_call_target="tpu_custom_call" | custom-call | tf_op jit(solution)/shard_map/diag_sum/pallas_call | solution.py:587
  167.3 2.6 %sub.20 = f32[4,256,256]{2,1,0:T(8,128)} subtract(f32[4,256,256]{2,1,0:T(8,128)} %param.10, f32[4,256,256]{2,1,0:T(8,128)} %bitcast.16) | non-fusion elementwise | flops 262144 | bytes 3145728 | tf_op jit(solution)/shard_map/sub | solution.py:604
  (8 shorter events, 0.1 us)

commit v2 on v0

v2 whole, which is shorter than its diff:
```python
import functools

import jax
import jax.numpy as jnp
from jax import lax
from jax.experimental import pallas as pl
from jax.experimental.pallas import tpu as pltpu
from jax.sharding import PartitionSpec as P

MESH = pl.DeviceIdType.MESH
F32 = jnp.float32
BF16 = jnp.bfloat16
KEEP = 36
FIRST = 24
QR = 3
STAGES = 4
ROWS = 128
LAGS = (1, 3, 5, 7)


def coords():
    k = lax.axis_index("prow")
    j = lax.axis_index("pcol")
    return k // 2, j // 4, (j // 2) % 2, k % 2, j % 2


def dev(x, y, zh, zl, c):
    return (x * 2 + zl, (y * 2 + zh) * 2 + c)


def split2(v):
    hi = v.astype(BF16)
    lo = (v - hi.astype(F32)).astype(BF16)
    return hi, lo


def valid_slots(block_lists, list_mask, slot_of_block):
    window_blocks = block_lists.shape[1]
    block_ids = jnp.arange(window_blocks, dtype=jnp.int32)
    chosen = (block_lists[:, :, None] == block_ids[None, None, :]).astype(jnp.int32)
    slot_ids = jnp.sum(chosen * slot_of_block[None, None, :], axis=2)
    matches = (slot_ids[:, :, None] == block_ids[None, None, :]).astype(jnp.int32) * list_mask[
        :, :, None
    ]
    return jnp.sum(matches, axis=1)


def packed_order(valid, group):
    v = lax.dynamic_slice_in_dim(valid, group * 12, 12, 1).reshape(48)
    i = jnp.arange(48, dtype=jnp.int32)
    pos = jnp.sum(v[None, :] * (i[None, :] < i[:, None]).astype(jnp.int32), axis=1)
    q = jnp.arange(KEEP, dtype=jnp.int32)
    hit = (pos[None, :] == q[:, None]).astype(jnp.int32) * v[None, :]
    idx = jnp.sum(hit * i[None, :], axis=1)
    return jnp.where(v > 0, pos, -1), idx


def prep_kernel(tab, f_ref, inv_ref, nc_ref, nd_ref):
    for p in range(4):
        nd_ref[p] = jnp.dot(
            f_ref[p].reshape(192, 256),
            inv_ref[p],
            precision=lax.Precision.HIGHEST,
            preferred_element_type=F32,
        ).reshape(12, 16, 256)

    @pl.loop(0, KEEP)
    def _(q):
        nc_ref[q] = nd_ref[tab[1, q], tab[0, q]]


def main_kernel(
    tab, g_hbm, nc, nd, given, pid, dout,
    out, ghi, glo, stage, ng0, ng1, nhi, nlo, pb, rc, ra, rb, rp, rm, rz, outx, ndt, pt, dw, e1, e2,
    g_sem, p1_s, p1_r, xp_s, xp_r, xm_s, xm_r, z_s, z_r, c_s, c_r, rs_s, rs_r, ar_s, ar_r,
):
    x, y, zh, zl, c = coords()
    z = 2 * zh + zl
    xp, xm, xf = (x + 1) % 4, (x + 3) % 4, (x + 2) % 4
    yp, ym, yf = (y + 1) % 4, (y + 3) % 4, (y + 2) % 4
    zn = 1 - zl
    d_xp, d_xm = dev(xp, y, zh, zl, c), dev(xm, y, zh, zl, c)
    d_zn, d_c = dev(x, y, zh, zn, c), dev(x, y, zh, zl, 1 - c)
    d_yp, d_ym = dev(x, yp, zh, zl, c), dev(x, ym, zh, zl, c)
    d_z2 = dev(x, y, 1 - zh, zl, c)
    d_to = dev((y + 2 * (x % 2)) % 4, x, zl, zh, c)
    d_from = dev(y, (x + 2 * (y % 2)) % 4, zl, zh, c)
    own_target = ((x == y) & (x % 2 == 0)) & (zl == zh)

    at = (jnp.where(c == 0, x, y), jnp.where(c == 0, y, x), z)

    def peer(n1, n2, n3):
        a, b, e = (at[0] + n1) % 4, (at[1] + n2) % 4, (at[2] + n3) % 4
        return dev(jnp.where(c == 0, a, b), jnp.where(c == 0, b, a), e // 2, e % 2, c)

    plane = [(n2, n3) for n2 in range(4) for n3 in range(4) if (n2, n3) != (0, 0)]

    barrier = pltpu.get_barrier_semaphore()
    for d in [d_c] + [peer(n, 0, 0) for n in (1, 2, 3)] + [peer(0, *n) for n in plane]:
        pl.semaphore_signal(barrier, inc=1, device_id=d, device_id_type=MESH)

    @pl.when(jnp.logical_not(own_target))
    def _():
        for d in (d_to, d_from):
            pl.semaphore_signal(barrier, inc=1, device_id=d, device_id_type=MESH)
        pl.semaphore_wait(barrier, 21)

    @pl.when(own_target)
    def _():
        pl.semaphore_wait(barrier, 19)

    def share(xx, zz):
        return 2 * (2 * ((xx + 2 * (y % 2)) % 4) + zz) + c

    r_me = (y * 2 + zh) * 2 + c
    s_o, s_l, s_r, s_f = (share(v, zl) for v in (x, xm, xp, xf))
    t_o, t_l, t_r, t_f = (share(v, zn) for v in (x, xm, xp, xf))
    cuts = ((0, 5, 10, 17, 24), (0, 3, 6, 9, 12))
    ng = (ng0, ng1)
    base = (0, FIRST)

    def rcopy(src, dst, ss, rs, d):
        return pltpu.make_async_remote_copy(
            src_ref=src, dst_ref=dst, send_sem=ss, recv_sem=rs, device_id=d, device_id_type=MESH
        )


    spans = tuple(((v[0], v[2]), (v[2], v[4])) for v in cuts)

    def p1(h, i):
        lo, hi = spans[h][i]
        return rcopy(
            nc.at[pl.ds(base[h] + lo, hi - lo)], ng[h].at[pl.ds(lo, hi - lo), r_me],
            p1_s.at[h, i], p1_r.at[h, i], d_to,
        )

    def p1_local(h, i):
        lo, hi = spans[h][i]
        return pltpu.make_async_copy(
            nc.at[pl.ds(base[h] + lo, hi - lo)], ng[h].at[pl.ds(lo, hi - lo), s_o], p1_r.at[h, i]
        )

    def m_rows():
        return rcopy(nd.at[pl.ds(2 * (1 - c), 2)], ndt, ar_s.at[0], ar_r.at[0], d_c)

    @pl.when(jnp.logical_not(own_target))
    def _():
        for h in (0, 1):
            for i in (0, 1):
                p1(h, i).start()

    @pl.when(own_target)
    def _():
        for h in (0, 1):
            for i in (0, 1):
                p1_local(h, i).start()

    def p1_wait(h, i):
        @pl.when(jnp.logical_not(own_target))
        def _():
            p1(h, i).wait_recv()

        @pl.when(own_target)
        def _():
            p1_local(h, i).wait()


    chunks = 3072 // ROWS

    def g_copy(i):
        slot = i % STAGES
        return pltpu.make_async_copy(
            g_hbm.at[pl.ds(i * ROWS, ROWS), :], stage.at[slot], g_sem.at[slot]
        )

    for n in range(STAGES - 1):
        g_copy(n).start()

    def load_g(i, carry):
        g_copy(i).wait()

        @pl.when(i < chunks - STAGES + 1)
        def _():
            g_copy(i + STAGES - 1).start()

        per = 256 // ROWS
        b, r0 = i // per, (i % per) * ROWS
        for r in range(0, ROWS, 64):
            hi, lo = split2(stage[i % STAGES, r : r + 64, :])
            at = pl.ds(pl.multiple_of(r0 + r, 64), 64)
            ghi[b, at, :] = hi
            glo[b, at, :] = lo
        return carry

    def some_g(lo, hi):
        lax.fori_loop(lo, hi, load_g, 0)


    to_xp = ((0, 2, s_o), (2, 4, s_o), (2, 4, t_o), (0, 1, s_l), (2, 3, s_l), (2, 3, t_l))
    to_xm = ((0, 2, s_o), (2, 4, s_o), (2, 4, t_o), (1, 2, s_r), (3, 4, s_r), (3, 4, t_r))
    to_z = ((0, 2, s_o), (2, 4, s_o), (0, 2, s_l), (0, 2, s_r), (0, 1, s_f), (1, 2, s_f))
    of_xm = ((0, 2, s_l), (2, 4, s_l), (2, 4, t_l), (0, 1, s_f), (2, 3, s_f), (2, 3, t_f))
    of_xp = ((0, 2, s_r), (2, 4, s_r), (2, 4, t_r), (1, 2, s_f), (3, 4, s_f), (3, 4, t_f))
    of_z = ((0, 2, t_o), (2, 4, t_o), (0, 2, t_l), (0, 2, t_r), (0, 1, t_f), (1, 2, t_f))
    order = (s_o, s_l, s_r, t_o, s_f, t_l, t_r, t_f)

    def go(h, table, sems, d, i):
        lo, hi, s = table[i]
        lo, hi = cuts[h][lo], cuts[h][hi]
        blocks = ng[h].at[pl.ds(lo, hi - lo), s]
        return rcopy(blocks, blocks, sems[0].at[h, i], sems[1].at[h, i], d)

    xps, xms, zs = (xp_s, xp_r), (xm_s, xm_r), (z_s, z_r)

    def twin(h, i, s):
        blocks = ng[h].at[:, s]
        return rcopy(blocks, blocks, c_s.at[h, i], c_r.at[h, i], d_c)

    def gather_steps(h):
        def send(*what):
            for name, i in what:
                if name == "xp":
                    go(h, to_xp, xps, d_xp, i).start()
                elif name == "xm":
                    go(h, to_xm, xms, d_xm, i).start()
                elif name == "z":
                    go(h, to_z, zs, d_zn, i).start()
                else:
                    twin(h, i, order[i]).start()

        def got(*what):
            for name, i in what:
                if name == "xm":
                    go(h, of_xm, xps, d_xp, i).wait_recv()
                elif name == "xp":
                    go(h, of_xp, xms, d_xm, i).wait_recv()
                else:
                    go(h, of_z, zs, d_zn, i).wait_recv()

        def first():
            p1_wait(h, 0)
            send(("xp", 0), ("xm", 0), ("z", 0))

        def second():
            p1_wait(h, 1)
            send(("xp", 1), ("xm", 1), ("z", 1), ("c", 0))

        def a_sides():
            got(("xm", 0))
            send(("xp", 3), ("z", 2))
            got(("xp", 0))
            send(("xm", 3), ("z", 3))

        def b_sides():
            got(("xm", 1))
            send(("xp", 4), ("c", 1))
            got(("xp", 1))
            send(("xm", 4), ("c", 2))

        def pair():
            got(("z", 0), ("z", 1))
            send(("xp", 2), ("xm", 2), ("c", 3))

        def far_a():
            got(("xm", 3))
            send(("z", 4))
            got(("xp", 3))
            send(("z", 5))

        def pair_sides():
            got(("xm", 2))
            send(("xp", 5))
            got(("xp", 2))
            send(("xm", 5))

        def far_b():
            got(("xm", 4), ("xp", 4))
            send(("c", 4))

        def last_sides():
            got(("z", 2))
            send(("c", 5))
            got(("z", 3))
            send(("c", 6))

        def last_far():
            got(("xm", 5), ("xp", 5), ("z", 4), ("z", 5))
            send(("c", 7))

        return (
            first, second, a_sides, b_sides, pair, far_a, pair_sides, far_b, last_sides, last_far,
        )

    def spread(h):
        for i in range(8):
            twin(h, i, order[i] + 1 - 2 * c).wait_recv()

        def block(i, carry):
            p, t = i // 6, i % 6
            w = tab[2, i]
            v = ng0[jnp.clip(w, 0, FIRST - 1)].reshape(256, 256)
            if h == 1:
                late = ng1[jnp.clip(w - FIRST, 0, KEEP - FIRST - 1)].reshape(256, 256)
                v = jnp.where(w >= FIRST, late, v)
            v = jnp.where(w >= 0, v, 0.0)
            hi, lo = split2(v)
            nhi[p, t] = hi
            nlo[p, t] = lo
            return carry

        lax.fori_loop(12 * h, 12 * h + 12, block, 0)


    rounds = KEEP // QR
    early = KEEP // 3 // QR

    def product(q):
        s, p = tab[0, q], tab[1, q]
        bh = nhi[p].reshape(1536, 256)
        v = jnp.dot(ghi[s], bh, preferred_element_type=F32)
        v += jnp.dot(ghi[s], nlo[p].reshape(1536, 256), preferred_element_type=F32)
        v += jnp.dot(glo[s], bh, preferred_element_type=F32)
        pb[q] = v.reshape(4, 2, 2, 16, 256)

    def m_core(g):
        qs = pl.ds(g * QR, QR)
        return rcopy(pb.at[qs, :, :, 1 - c], rc.at[qs], rs_s.at[0, g], rs_r.at[0, g], d_c)

    def m_a(g):
        qs = pl.ds(g * QR, QR)
        return rcopy(pb.at[qs, yf, 0, c], ra.at[qs], rs_s.at[1, g], rs_r.at[1, g], d_yp)

    def m_b(g):
        qs = pl.ds(g * QR, QR)
        return rcopy(pb.at[qs, yf, 1, c], rb.at[qs], rs_s.at[2, g], rs_r.at[2, g], d_ym)

    def m_p(g):
        qs = pl.ds(g * QR, QR)
        return rcopy(pb.at[qs, yp, :, c], rp.at[qs], rs_s.at[3, g], rs_r.at[3, g], d_yp)

    def m_m(g):
        qs = pl.ds(g * QR, QR)
        return rcopy(pb.at[qs, ym, :, c], rm.at[qs], rs_s.at[4, g], rs_r.at[4, g], d_ym)

    def m_z(g):
        qs = pl.ds(g * QR, QR)
        return rcopy(pb.at[qs, y, 1 - zh, c], rz.at[qs], rs_s.at[5, g], rs_r.at[5, g], d_z2)

    def m_out(g):
        qs = pl.ds(g * QR, QR)
        return rcopy(out.at[qs], outx.at[qs], rs_s.at[6, g], rs_r.at[6, g], d_c)


    def m_down(n):
        return rcopy(
            dw.at[(at[0] + n) % 4], e1.at[n - 1], ar_s.at[n], ar_r.at[n], peer(n, 0, 0)
        )

    def m_plane(n2, n3):
        k = n2 * 4 + n3
        return rcopy(
            dw.at[at[0], (at[1] + n2) % 4, (at[2] + n3) % 4], e2.at[k - 1],
            ar_s.at[3 + k], ar_r.at[3 + k], peer(0, n2, n3),
        )

    def m_plane_up(n2, n3):
        k = n2 * 4 + n3
        part = dout.at[c, at[0], at[1], at[2]]
        return rcopy(part, part, ar_s.at[18 + k], ar_r.at[18 + k], peer(0, n2, n3))

    def m_up(n):
        part = dout.at[c, at[0]]
        return rcopy(part, part, ar_s.at[33 + n], ar_r.at[33 + n], peer(n, 0, 0))

    def m_twin(n):
        part = dout.at[c, (at[0] + 4 - n) % 4]
        return rcopy(part, part, ar_s.at[37 + n], ar_r.at[37 + n], d_c)

    def diagonal():
        for p in range(4):
            for s in range(12):
                w = tab[3, p * 12 + s]
                pid[p, s] = jnp.where(w >= 0, out[jnp.maximum(w, 0)], 0.0)
        m_rows().wait_recv()

        @pl.loop(0, rounds)
        def _(g):
            m_out(g).wait_recv()

        def term(a, b):
            return lax.dot_general(
                a.reshape(192, 256), b.reshape(192, 256), (((0,), (0,)), ((), ())),
                precision=lax.Precision.HIGHEST, preferred_element_type=F32,
            )

        for k in range(2):
            p = 2 * c + k
            for s in range(12):
                w = tab[3, p * 12 + s]
                pt[s] = jnp.where(w >= 0, outx[jnp.maximum(w, 0)], 0.0)
            d = term(nd[p], pid[p]) + term(ndt[k], pt[...])
            dw[2 * k : 2 * k + 2] = d.reshape(2, 4, 4, 8, 256)
        for n in (1, 3, 2):
            m_down(n).start()
        for n in (1, 3, 2):
            m_down(n).wait_recv()
        dw[at[0]] = dw[at[0]] + (e1[0] + e1[1] + e1[2])
        for n in plane:
            m_plane(*n).start()
        for n in plane:
            m_plane(*n).wait_recv()
        total = dw[at[0], at[1], at[2]]
        for k in range(15):
            total = total + e2[k]
        dout[c, at[0], at[1], at[2]] = given[c, at[0], at[1], at[2]] - total
        for n in plane:
            m_plane_up(*n).start()
        for n in plane:
            m_plane_up(*n).wait_recv()
        for n in (1, 3, 2):
            m_up(n).start()
        m_twin(0).start()
        for n in (1, 3, 2):
            m_up(n).wait_recv()
            m_twin(n).start()
        for n in range(4):
            m_twin(n).wait_recv()

    def diagonal_sent():
        m_rows().wait_send()
        for n in (1, 2, 3):
            m_down(n).wait_send()
            m_up(n).wait_send()
        for n in plane:
            m_plane(*n).wait_send()
            m_plane_up(*n).wait_send()
        for n in range(4):
            m_twin(n).wait_send()


    one, two = gather_steps(0), gather_steps(1)
    m_rows().start()
    some_g(0, G_FIRST)
    one[0]()
    some_g(G_FIRST, G_FIRST + 2)
    one[1]()
    left = chunks - G_FIRST - 2
    for n in range(2, 7):
        some_g(G_FIRST + 2 + left * (n - 2) // 5, G_FIRST + 2 + left * (n - 1) // 5)
        one[n]()
    two[0]()
    two[1]()
    for n in range(7, 10):
        one[n]()
    spread(0)

    under = {}
    for n, r in zip(range(2, 10), GATHER_AT):
        under.setdefault(r, []).append(two[n])
    under.setdefault(early, []).append(lambda: spread(1))

    def step(i, carry):
        for r, acts in under.items():

            @pl.when(i == r)
            def _(acts=acts):
                for act in acts:
                    act()

        @pl.when(i < rounds)
        def _():
            @pl.loop(0, QR)
            def _(n):
                product(i * QR + n)

            m_core(i).start()

        @pl.when((i >= LAGS[0]) & (i < rounds + LAGS[0]))
        def _():
            g = i - LAGS[0]
            m_core(g).wait_recv()

            @pl.loop(0, QR)
            def _(n):
                q = g * QR + n
                pb[q, :, :, c] += rc[q]

            m_a(g).start()
            m_b(g).start()

        @pl.when((i >= LAGS[1]) & (i < rounds + LAGS[1]))
        def _():
            g = i - LAGS[1]
            m_a(g).wait_recv()
            m_b(g).wait_recv()

            @pl.loop(0, QR)
            def _(n):
                q = g * QR + n
                pb[q, yp, 0, c] += ra[q]
                pb[q, ym, 1, c] += rb[q]

            m_p(g).start()
            m_m(g).start()

        @pl.when((i >= LAGS[2]) & (i < rounds + LAGS[2]))
        def _():
            g = i - LAGS[2]
            m_p(g).wait_recv()
            m_m(g).wait_recv()

            @pl.loop(0, QR)
            def _(n):
                q = g * QR + n
                pb[q, y, :, c] += rp[q] + rm[q]

            m_z(g).start()

        @pl.when(i >= LAGS[3])
        def _():
            g = i - LAGS[3]
            m_z(g).wait_recv()

            @pl.loop(0, QR)
            def _(n):
                q = g * QR + n
                out[q] = -(pb[q, y, zh, c] + rz[q])

            m_out(g).start()

        return carry

    lax.fori_loop(0, rounds + LAGS[3], step, 0)
    diagonal()

    @pl.when(jnp.logical_not(own_target))
    def _():
        for h in (0, 1):
            p1(h, 0).wait_send()
            p1(h, 1).wait_send()

    for h in (0, 1):
        for i in range(6):
            go(h, to_xp, xps, d_xp, i).wait_send()
            go(h, to_xm, xms, d_xm, i).wait_send()
            go(h, to_z, zs, d_zn, i).wait_send()
        for i in range(8):
            twin(h, i, order[i]).wait_send()

    @pl.loop(0, rounds)
    def _(g):
        m_core(g).wait_send()
        m_a(g).wait_send()
        m_b(g).wait_send()
        m_p(g).wait_send()
        m_m(g).wait_send()
        m_z(g).wait_send()
        m_out(g).wait_send()

    diagonal_sent()


VM = pl.BlockSpec(memory_space=pltpu.VMEM)
SM = pl.BlockSpec(memory_space=pltpu.SMEM)
ANY = pl.BlockSpec(memory_space=pl.ANY)
DMA = pltpu.SemaphoreType.DMA
G_FIRST = 10
GATHER_AT = (1, 1, 2, 2, 3, 3, 4, 4)


def on_device(
    inverse_matrix, factor_blocks, factor_inverse, diag_given, block_lists, list_mask, slot_of_block
):
    k = lax.axis_index("prow")
    j = lax.axis_index("pcol")
    valid = valid_slots(block_lists, list_mask, slot_of_block)
    pos_row, idx = packed_order(valid, k)
    pos_col, _ = packed_order(valid, j // 2)
    s_q = idx % 12
    p_q = idx // 12
    col = lax.dynamic_slice_in_dim(pos_col.reshape(4, 12), (j % 2) * 6, 6, 1).reshape(24)
    tab = jnp.stack(
        [jnp.pad(s_q, (0, 12)), jnp.pad(p_q, (0, 12)), jnp.pad(col, (0, 24)), pos_row]
    )

    nc, nd = pl.pallas_call(
        prep_kernel,
        out_shape=(
            jax.ShapeDtypeStruct((KEEP, 16, 256), F32),
            jax.ShapeDtypeStruct((4, 12, 16, 256), F32),
        ),
        in_specs=[SM, VM, VM],
        out_specs=(VM, VM),
        name="normalize",
    )(tab, factor_blocks, factor_inverse)

    rounds = KEEP // QR
    panel_inverse, diag = pl.pallas_call(
        main_kernel,
        out_shape=(
            jax.ShapeDtypeStruct((4, 12, 16, 256), F32),
            jax.ShapeDtypeStruct((2, 4, 4, 4, 8, 256), F32),
        ),
        in_specs=[SM, ANY, VM, VM, VM],
        out_specs=(VM, VM),
        scratch_shapes=[
            pltpu.VMEM((KEEP, 16, 256), F32),
            pltpu.VMEM((12, 256, 1536), BF16),
            pltpu.VMEM((12, 256, 1536), BF16),
            pltpu.VMEM((STAGES, ROWS, 1536), F32),
            pltpu.VMEM((FIRST, 16, 16, 256), F32),
            pltpu.VMEM((KEEP - FIRST, 16, 16, 256), F32),
            pltpu.VMEM((4, 6, 256, 256), BF16),
            pltpu.VMEM((4, 6, 256, 256), BF16),
            pltpu.VMEM((KEEP, 4, 2, 2, 16, 256), F32),
            pltpu.VMEM((KEEP, 4, 2, 16, 256), F32),
            pltpu.VMEM((KEEP, 16, 256), F32),
            pltpu.VMEM((KEEP, 16, 256), F32),
            pltpu.VMEM((KEEP, 2, 16, 256), F32),
            pltpu.VMEM((KEEP, 2, 16, 256), F32),
            pltpu.VMEM((KEEP, 16, 256), F32),
            pltpu.VMEM((KEEP, 16, 256), F32),
            pltpu.VMEM((2, 12, 16, 256), F32),
            pltpu.VMEM((12, 16, 256), F32),
            pltpu.VMEM((4, 4, 4, 8, 256), F32),
            pltpu.VMEM((3, 4, 4, 8, 256), F32),
            pltpu.VMEM((15, 8, 256), F32),
            DMA((STAGES,)),
            DMA((2, 2)),
            DMA((2, 2)),
            DMA((2, 6)),
            DMA((2, 6)),
            DMA((2, 6)),
            DMA((2, 6)),
            DMA((2, 6)),
            DMA((2, 6)),
            DMA((2, 8)),
            DMA((2, 8)),
            DMA((7, rounds)),
            DMA((7, rounds)),
            DMA((41,)),
            DMA((41,)),
        ],
        compiler_params=pltpu.CompilerParams(
            collective_id=0, has_side_effects=True, vmem_limit_bytes=67043328
        ),
        name="window",
    )(tab, inverse_matrix, nc, nd, diag_given.reshape(2, 4, 4, 4, 8, 256))
    return (panel_inverse, diag.reshape(4, 256, 256))


def solution(mesh):
    return jax.shard_map(
        on_device,
        mesh=mesh,
        in_specs=(P("prow", "pcol"), P(None, "prow", "pcol", None), P(), P(), P(), P(), P()),
        out_specs=(P(None, "prow", "pcol", None), P()),
        check_vma=False,
    )
```

time: 628 us -> 149 us (0.24)
  waiting for transfers between devices: 367 us -> 0 us
  Pallas kernels: 0 us -> 140 us
  matrix products: 131 us -> 0 us
  blocking collectives: 89.8 us -> 0 us
  local copies, waits for them, and re-layouts: 19.1 us -> 4.93 us
  between operations: 13.9 us -> 0.72 us
    psum x1 -> x0, waiting for transfers between devices: 148 us -> none  [on_device(): diag_inverse = diag_given - lax.psum(local_diag, PROW_PCOL)]
    pallas_call x0 -> x2, Pallas kernels: none -> 140 us  [the longest x1 136 us: on_device(): pl.pallas_call(main_kernel, out_shape=(jax.ShapeDtypeStruct((4, 12, 16, 2...]
    dot_general x3 -> x0, matrix products: 131 us -> none  [the longest x1 125 us: on_device(): jnp.einsum('ij,pjk->pik', inverse_matrix, stacked, precision=highest, pre...]
    reduce_scatter x1 -> x0, waiting for transfers between devices: 118 us -> none  [on_device(): lax.psum_scatter(partial_value, 'pcol', scatter_dimension=2, tiled=True)]
    all_gather x2 -> x0, waiting for transfers between devices: 101 us -> none  [whole_of(): array = lax.all_gather(array, axis, axis=dim, tiled=True)]
    all_to_all x2 -> x0, blocking collectives: 89.8 us -> none  [cut_exchange(): lax.all_to_all(share, axis, split_axis=0, concat_axis=0, tiled=True)]
    transpose x1 -> x0, local copies, waits for them, and re-layouts: 12.6 us -> none  [on_device(): jnp.einsum('ij,pjk->pik', inverse_matrix, stacked, precision=highest, pre...]
  transfers between devices with their start and end apart: 4 -> 0, of which waited for: 4 -> 0; matrix products, arithmetic and copies ran while one was open for 0% -> 0% of each run, Pallas kernels for 0% -> 0%
where the time goes in v2:
time: 149 us
  Pallas kernels  140 us (94%)
  local copies, waits for them, and re-layouts  4.93 us (3%)
  other arithmetic  2.92 us (2%)
    pallas_call x1, Pallas kernels, on_device(): pl.pallas_call(main_kernel, out_shape=(jax.ShapeDtypeStruct((4, 12, 16, 2...  136 us
    unnamed x2, local copies, waits for them, and re-layouts  4.35 us
    pallas_call x1, Pallas kernels, on_device(): pl.pallas_call(prep_kernel, out_shape=(jax.ShapeDtypeStruct((KEEP, 16, 25...  3.8 us

profile of v2, /device:TPU:1, one launch (start us, length us, event | category | flops | bytes accessed | tf_op | source)
XLA Modules:
  0.0 148.6 jit_solution(16700437135327404105)
XLA Ops:
  0.7 0.9 select_reduce_fusion.1
  1.6 0.9 select_reduce_fusion
  2.5 0.1 constant_dynamic-slice_fusion
  2.5 0.1 mul.74
  2.6 0.1 select_reduce_fusion.2
  2.7 0.1 reduce_sum.54
  2.8 0.1 compare_select_fusion
  2.9 0.1 constant_dynamic-slice_fusion.1
  3.0 0.1 reshape.43
  3.1 0.1 broadcast_compare_fusion
  3.1 0.1 gt.19
  3.2 0.1 mul.66
  3.3 0.1 select_reduce_fusion.3
  3.4 0.1 multiply_reduce_fusion
  3.6 0.6 pad_add_fusion.tab
  4.2 3.8 %normalize.1 = (f32[36,16,256]{2,1,0:T(8,128)}, f32[4,12,16,256]{3,2,1,0:T(8,128)}) custom-call(s32[4,48]{1,0:T(4,128)} %pad_add_fusion.tab, f32[4,12,16,256]{3,2,1,0:T(8,128)} %f_ref.1, f32[4,256,256]{2,1,0:T(8,128)} %inv_ref.1), custom_call_target="tpu_custom_call" | custom-call | tf_op jit(solution)/shard_map/normalize/pallas_call | solution.py:586
  8.0 136.2 %window.1 = (f32[4,12,16,256]{3,2,1,0:T(8,128)}, f32[2,4,4,4,8,256]{5,4,3,2,1,0:T(8,128)}) custom-call(s32[4,48]{1,0:T(4,128)} %pad_add_fusion.tab, f32[3072,1536]{1,0:T(8,128)} %g_hbm.1, f32[36,16,256]{2,1,0:T(8,128)} %get-tuple-element.6.nc, f32[4,12,16,256]{3,2,1,0:T(8,128)} %get-tuple-element.7.nd, f32[2,4,4,4,8,256]{5,4,3,2,1,0:T(8,128)} %bitcast.10), custom_call_target="tpu_custom_call" | custom-call | tf_op jit(solution)/shard_map/window/pallas_call | solution.py:598
  144.2 2.1 %copy.11 = f32[4,12,16,256]{3,2,1,0:T(8,128)} copy(f32[4,12,16,256]{3,2,1,0:T(8,128)} %get-tuple-element.18) | data formatting | bytes 1572864
  146.3 2.3 %copy.12 = f32[4,256,256]{2,1,0:T(8,128)} copy(f32[4,256,256]{2,1,0:T(8,128)} %bitcast.11) | data formatting | bytes 2097152
  (4 shorter events, 0.0 us)

commit v3 on v2

--- a/solution.py
+++ b/solution.py
@@ -55,24 +55,10 @@
     return jnp.where(v > 0, pos, -1), idx
 
 
-def prep_kernel(tab, f_ref, inv_ref, nc_ref, nd_ref):
-    for p in range(4):
-        nd_ref[p] = jnp.dot(
-            f_ref[p].reshape(192, 256),
-            inv_ref[p],
-            precision=lax.Precision.HIGHEST,
-            preferred_element_type=F32,
-        ).reshape(12, 16, 256)
-
-    @pl.loop(0, KEEP)
-    def _(q):
-        nc_ref[q] = nd_ref[tab[1, q], tab[0, q]]
-
-
 def main_kernel(
-    tab, g_hbm, nc, nd, given, pid, dout,
-    out, ghi, glo, stage, ng0, ng1, nhi, nlo, pb, rc, ra, rb, rp, rm, rz, outx, ndt, pt, dw, e1, e2,
-    g_sem, p1_s, p1_r, xp_s, xp_r, xm_s, xm_r, z_s, z_r, c_s, c_r, rs_s, rs_r, ar_s, ar_r,
+    tab, g_hbm, f_hbm, inv_hbm, given, pid, dout,
+    nd, inv, nc, gv, out, ghi, glo, stage, ng0, ng1, nhi, nlo, pb, rc, ra, rb, rp, rm, rz, outx, ndt, pt, dw, dsum, e1, e2,
+    in_sem, g_sem, p1_s, p1_r, xp_s, xp_r, xm_s, xm_r, z_s, z_r, c_s, c_r, rs_s, rs_r, ar_s, ar_r,
 ):
     x, y, zh, zl, c = coords()
     z = 2 * zh + zl
@@ -103,6 +89,42 @@
     def _():
         for d in (d_to, d_from):
             pl.semaphore_signal(barrier, inc=1, device_id=d, device_id_type=MESH)
+
+    ins = (
+        pltpu.make_async_copy(f_hbm, nd, in_sem.at[0]),
+        pltpu.make_async_copy(inv_hbm, inv, in_sem.at[1]),
+        pltpu.make_async_copy(given.at[c, at[0], at[1], at[2]], gv, in_sem.at[2]),
+    )
+    for cp in ins:
+        cp.start()
+
+    chunks = 3072 // ROWS
+
+    def g_copy(i):
+        slot = i % STAGES
+        return pltpu.make_async_copy(
+            g_hbm.at[pl.ds(i * ROWS, ROWS), :], stage.at[slot], g_sem.at[slot]
+        )
+
+    for n in range(STAGES - 1):
+        g_copy(n).start()
+
+    for cp in ins:
+        cp.wait()
+    for p in range(4):
+        nd[p] = jnp.dot(
+            nd[p].reshape(192, 256),
+            inv[p],
+            precision=lax.Precision.HIGHEST,
+            preferred_element_type=F32,
+        ).reshape(12, 16, 256)
+
+    @pl.loop(0, KEEP)
+    def _(q):
+        nc[q] = nd[tab[1, q], tab[0, q]]
+
+    @pl.when(jnp.logical_not(own_target))
+    def _():
         pl.semaphore_wait(barrier, 21)
 
     @pl.when(own_target)
@@ -141,18 +163,18 @@
         )
 
     def m_rows():
-        return rcopy(nd.at[pl.ds(2 * (1 - c), 2)], ndt, ar_s.at[0], ar_r.at[0], d_c)
+        return rcopy(nd.at[pl.ds(2 * (1 - c), 2)], ndt, ar_s.at[0, 0], ar_r.at[0, 0], d_c)
 
     @pl.when(jnp.logical_not(own_target))
     def _():
         for h in (0, 1):
-            for i in (0, 1):
+            for i in (1, 0):
                 p1(h, i).start()
 
     @pl.when(own_target)
     def _():
         for h in (0, 1):
-            for i in (0, 1):
+            for i in (1, 0):
                 p1_local(h, i).start()
 
     def p1_wait(h, i):
@@ -164,17 +186,6 @@
         def _():
             p1_local(h, i).wait()
 
-
-    chunks = 3072 // ROWS
-
-    def g_copy(i):
-        slot = i % STAGES
-        return pltpu.make_async_copy(
-            g_hbm.at[pl.ds(i * ROWS, ROWS), :], stage.at[slot], g_sem.at[slot]
-        )
-
-    for n in range(STAGES - 1):
-        g_copy(n).start()
 
     def load_g(i, carry):
         g_copy(i).wait()
@@ -238,34 +249,32 @@
                     go(h, of_z, zs, d_zn, i).wait_recv()
 
         def first():
+            p1_wait(h, 1)
+            send(("xp", 1), ("xm", 1), ("z", 1))
+
+        def second():
             p1_wait(h, 0)
-            send(("xp", 0), ("xm", 0), ("z", 0))
-
-        def second():
-            p1_wait(h, 1)
-            send(("xp", 1), ("xm", 1), ("z", 1), ("c", 0))
+            send(("xp", 0), ("xm", 0), ("z", 0), ("c", 0))
+
+        def b_sides():
+            got(("xm", 1))
+            send(("xp", 4))
+            got(("xp", 1))
+            send(("xm", 4))
+
+        def b_pair():
+            got(("z", 1))
+            send(("xp", 2), ("xm", 2))
 
         def a_sides():
             got(("xm", 0))
-            send(("xp", 3), ("z", 2))
+            send(("xp", 3), ("z", 2), ("c", 1))
             got(("xp", 0))
-            send(("xm", 3), ("z", 3))
-
-        def b_sides():
-            got(("xm", 1))
-            send(("xp", 4), ("c", 1))
-            got(("xp", 1))
-            send(("xm", 4), ("c", 2))
-
-        def pair():
-            got(("z", 0), ("z", 1))
-            send(("xp", 2), ("xm", 2), ("c", 3))
-
-        def far_a():
-            got(("xm", 3))
-            send(("z", 4))
-            got(("xp", 3))
-            send(("z", 5))
+            send(("xm", 3), ("z", 3), ("c", 2))
+
+        def a_pair():
+            got(("z", 0))
+            send(("c", 3))
 
         def pair_sides():
             got(("xm", 2))
@@ -273,9 +282,11 @@
             got(("xp", 2))
             send(("xm", 5))
 
-        def far_b():
-            got(("xm", 4), ("xp", 4))
-            send(("c", 4))
+        def far():
+            got(("xm", 4), ("xp", 4), ("xm", 3))
+            send(("z", 4))
+            got(("xp", 3))
+            send(("z", 5), ("c", 4))
 
         def last_sides():
             got(("z", 2))
@@ -288,7 +299,7 @@
             send(("c", 7))
 
         return (
-            first, second, a_sides, b_sides, pair, far_a, pair_sides, far_b, last_sides, last_far,
+            first, second, b_sides, b_pair, a_sides, a_pair, pair_sides, far, last_sides, last_far,
         )
 
     def spread(h):
@@ -351,30 +362,30 @@
         return rcopy(out.at[qs], outx.at[qs], rs_s.at[6, g], rs_r.at[6, g], d_c)
 
 
-    def m_down(n):
+    def m_down(n, w):
         return rcopy(
-            dw.at[(at[0] + n) % 4], e1.at[n - 1], ar_s.at[n], ar_r.at[n], peer(n, 0, 0)
+            dw.at[w, (at[0] + n) % 4], e1.at[w, n - 1], ar_s.at[w, n], ar_r.at[w, n], peer(n, 0, 0)
         )
 
-    def m_plane(n2, n3):
+    def m_plane(n2, n3, w):
         k = n2 * 4 + n3
         return rcopy(
-            dw.at[at[0], (at[1] + n2) % 4, (at[2] + n3) % 4], e2.at[k - 1],
-            ar_s.at[3 + k], ar_r.at[3 + k], peer(0, n2, n3),
+            dw.at[w, at[0], (at[1] + n2) % 4, (at[2] + n3) % 4], e2.at[w, k - 1],
+            ar_s.at[w, 3 + k], ar_r.at[w, 3 + k], peer(0, n2, n3),
         )
 
-    def m_plane_up(n2, n3):
+    def m_plane_up(n2, n3, w):
         k = n2 * 4 + n3
-        part = dout.at[c, at[0], at[1], at[2]]
-        return rcopy(part, part, ar_s.at[18 + k], ar_r.at[18 + k], peer(0, n2, n3))
-
-    def m_up(n):
-        part = dout.at[c, at[0]]
-        return rcopy(part, part, ar_s.at[33 + n], ar_r.at[33 + n], peer(n, 0, 0))
-
-    def m_twin(n):
-        part = dout.at[c, (at[0] + 4 - n) % 4]
-        return rcopy(part, part, ar_s.at[37 + n], ar_r.at[37 + n], d_c)
+        part = dsum.at[w, c, at[0], at[1], at[2]]
+        return rcopy(part, part, ar_s.at[w, 18 + k], ar_r.at[w, 18 + k], peer(0, n2, n3))
+
+    def m_up(n, w):
+        part = dsum.at[w, c, at[0]]
+        return rcopy(part, part, ar_s.at[w, 33 + n], ar_r.at[w, 33 + n], peer(n, 0, 0))
+
+    def m_twin(n, w):
+        part = dsum.at[w, c, (at[0] + 4 - n) % 4]
+        return rcopy(part, part, ar_s.at[w, 37 + n], ar_r.at[w, 37 + n], d_c)
 
     def diagonal():
         for p in range(4):
@@ -399,43 +410,53 @@
                 w = tab[3, p * 12 + s]
                 pt[s] = jnp.where(w >= 0, outx[jnp.maximum(w, 0)], 0.0)
             d = term(nd[p], pid[p]) + term(ndt[k], pt[...])
-            dw[2 * k : 2 * k + 2] = d.reshape(2, 4, 4, 8, 256)
-        for n in (1, 3, 2):
-            m_down(n).start()
-        for n in (1, 3, 2):
-            m_down(n).wait_recv()
-        dw[at[0]] = dw[at[0]] + (e1[0] + e1[1] + e1[2])
-        for n in plane:
-            m_plane(*n).start()
-        for n in plane:
-            m_plane(*n).wait_recv()
-        total = dw[at[0], at[1], at[2]]
-        for k in range(15):
-            total = total + e2[k]
-        dout[c, at[0], at[1], at[2]] = given[c, at[0], at[1], at[2]] - total
-        for n in plane:
-            m_plane_up(*n).start()
-        for n in plane:
-            m_plane_up(*n).wait_recv()
-        for n in (1, 3, 2):
-            m_up(n).start()
-        m_twin(0).start()
-        for n in (1, 3, 2):
-            m_up(n).wait_recv()
-            m_twin(n).start()
-        for n in range(4):
-            m_twin(n).wait_recv()
+            for w in (0, 1):
+                dw[w, 2 * k : 2 * k + 2] = d[:, 128 * w : 128 * w + 128].reshape(2, 4, 4, 8, 128)
+        both = (0, 1)
+        for w in both:
+            for n in (1, 3, 2):
+                m_down(n, w).start()
+        for w in both:
+            for n in (1, 3, 2):
+                m_down(n, w).wait_recv()
+            dw[w, at[0]] = dw[w, at[0]] + (e1[w, 0] + e1[w, 1] + e1[w, 2])
+            for n in plane:
+                m_plane(*n, w).start()
+        for w in both:
+            for n in plane:
+                m_plane(*n, w).wait_recv()
+            total = dw[w, at[0], at[1], at[2]]
+            for k in range(15):
+                total = total + e2[w, k]
+            dsum[w, c, at[0], at[1], at[2]] = gv[:, 128 * w : 128 * w + 128] - total
+            for n in plane:
+                m_plane_up(*n, w).start()
+        for w in both:
+            for n in plane:
+                m_plane_up(*n, w).wait_recv()
+            for n in (1, 3, 2):
+                m_up(n, w).start()
+            m_twin(0, w).start()
+        for w in both:
+            for n in (1, 3, 2):
+                m_up(n, w).wait_recv()
+                m_twin(n, w).start()
+        for w in both:
+            for n in range(4):
+                m_twin(n, w).wait_recv()
+            dout[:, :, :, :, :, 128 * w : 128 * w + 128] = dsum[w]
 
     def diagonal_sent():
         m_rows().wait_send()
-        for n in (1, 2, 3):
-            m_down(n).wait_send()
-            m_up(n).wait_send()
-        for n in plane:
-            m_plane(*n).wait_send()
-            m_plane_up(*n).wait_send()
-        for n in range(4):
-            m_twin(n).wait_send()
+        for w in (0, 1):
+            for n in (1, 2, 3):
+                m_down(n, w).wait_send()
+                m_up(n, w).wait_send()
+            for n in plane:
+                m_plane(*n, w).wait_send()
+                m_plane_up(*n, w).wait_send()
+            for n in range(4):
+                m_twin(n, w).wait_send()
 
 
     one, two = gather_steps(0), gather_steps(1)
@@ -560,6 +581,11 @@
     diagonal_sent()
 
 
+def results_kernel(a, b, a_out, b_out):
+    a_out[...] = a[...]
+    b_out[...] = b[...]
+
+
 VM = pl.BlockSpec(memory_space=pltpu.VMEM)
 SM = pl.BlockSpec(memory_space=pltpu.SMEM)
 ANY = pl.BlockSpec(memory_space=pl.ANY)
@@ -583,27 +609,20 @@
         [jnp.pad(s_q, (0, 12)), jnp.pad(p_q, (0, 12)), jnp.pad(col, (0, 24)), pos_row]
     )
 
-    nc, nd = pl.pallas_call(
-        prep_kernel,
-        out_shape=(
-            jax.ShapeDtypeStruct((KEEP, 16, 256), F32),
-            jax.ShapeDtypeStruct((4, 12, 16, 256), F32),
-        ),
-        in_specs=[SM, VM, VM],
-        out_specs=(VM, VM),
-        name="normalize",
-    )(tab, factor_blocks, factor_inverse)
-
     rounds = KEEP // QR
-    panel_inverse, diag = pl.pallas_call(
+    results = pl.pallas_call(
         main_kernel,
         out_shape=(
             jax.ShapeDtypeStruct((4, 12, 16, 256), F32),
             jax.ShapeDtypeStruct((2, 4, 4, 4, 8, 256), F32),
         ),
-        in_specs=[SM, ANY, VM, VM, VM],
+        in_specs=[SM, ANY, ANY, ANY, ANY],
         out_specs=(VM, VM),
         scratch_shapes=[
+            pltpu.VMEM((4, 12, 16, 256), F32),
+            pltpu.VMEM((4, 256, 256), F32),
+            pltpu.VMEM((KEEP, 16, 256), F32),
+            pltpu.VMEM((8, 256), F32),
             pltpu.VMEM((KEEP, 16, 256), F32),
             pltpu.VMEM((12, 256, 1536), BF16),
             pltpu.VMEM((12, 256, 1536), BF16),
@@ -622,9 +641,11 @@
             pltpu.VMEM((KEEP, 16, 256), F32),
             pltpu.VMEM((2, 12, 16, 256), F32),
             pltpu.VMEM((12, 16, 256), F32),
-            pltpu.VMEM((4, 4, 4, 8, 256), F32),
-            pltpu.VMEM((3, 4, 4, 8, 256), F32),
-            pltpu.VMEM((15, 8, 256), F32),
+            pltpu.VMEM((2, 4, 4, 4, 8, 128), F32),
+            pltpu.VMEM((2, 2, 4, 4, 4, 8, 128), F32),
+            pltpu.VMEM((2, 3, 4, 4, 8, 128), F32),
+            pltpu.VMEM((2, 15, 8, 128), F32),
+            DMA((3,)),
             DMA((STAGES,)),
             DMA((2, 2)),
             DMA((2, 2)),
@@ -638,14 +659,21 @@
             DMA((2, 8)),
             DMA((7, rounds)),
             DMA((7, rounds)),
-            DMA((41,)),
-            DMA((41,)),
+            DMA((2, 41)),
+            DMA((2, 41)),
         ],
         compiler_params=pltpu.CompilerParams(
             collective_id=0, has_side_effects=True, vmem_limit_bytes=67043328
         ),
         name="window",
-    )(tab, inverse_matrix, nc, nd, diag_given.reshape(2, 4, 4, 4, 8, 256))
+    )(tab, inverse_matrix, factor_blocks, factor_inverse, diag_given.reshape(2, 4, 4, 4, 8, 256))
+    panel_inverse, diag = pl.pallas_call(
+        results_kernel,
+        out_shape=tuple(jax.ShapeDtypeStruct(v.shape, F32) for v in results),
+        in_specs=[VM, VM],
+        out_specs=(VM, VM),
+        name="results",
+    )(*results)
     return (panel_inverse, diag.reshape(4, 256, 256))
 
 

time: 149 us -> 145 us (0.973)
  local copies, waits for them, and re-layouts: 4.93 us -> 0.58 us
    unnamed x2 -> x0, local copies, waits for them, and re-layouts: 4.35 us -> none
where the time goes in v3:
time: 145 us; the launch traced here: 144 us
  Pallas kernels  140 us (97%)
  other arithmetic  2.91 us (2%)
    pallas_call x1, Pallas kernels, on_device(): pl.pallas_call(main_kernel, out_shape=(jax.ShapeDtypeStruct((4, 12, 16, 2...  137 us

profile of v3, /device:TPU:1, one launch (start us, length us, event | category | flops | bytes accessed | tf_op | source)
XLA Modules:
  0.0 144.3 jit_solution(11537733481146690406)
XLA Ops:
  0.7 0.9 select_reduce_fusion.1
  1.6 0.9 select_reduce_fusion
  2.5 0.1 constant_dynamic-slice_fusion
  2.5 0.1 mul.74
  2.6 0.1 select_reduce_fusion.2
  2.7 0.1 reduce_sum.54
  2.8 0.1 compare_select_fusion
  2.9 0.1 constant_dynamic-slice_fusion.1
  3.0 0.1 reshape.43
  3.1 0.1 broadcast_compare_fusion
  3.1 0.1 gt.19
  3.2 0.1 mul.66
  3.3 0.1 select_reduce_fusion.3
  3.4 0.1 multiply_reduce_fusion
  3.6 0.6 pad_add_fusion.tab
  4.2 137.4 %window.1 = (f32[4,12,16,256]{3,2,1,0:T(8,128)}, f32[2,4,4,4,8,256]{5,4,3,2,1,0:T(8,128)}) custom-call(s32[4,48]{1,0:T(4,128)} %pad_add_fusion.tab, f32[3072,1536]{1,0:T(8,128)} %g_hbm.1, f32[4,12,16,256]{3,2,1,0:T(8,128)} %f_hbm.1, f32[4,256,256]{2,1,0:T(8,128)} %inv_hbm.1, f32[2,4,4,4,8,256]{5,4,3,2,1,0:T(8,128)} %bitcast.10), custom_call_target="tpu_custom_call" | custom-call | tf_op jit(solution)/shard_map/window/pallas_call | solution.py:613
  141.6 2.7 %results.1 = (f32[4,12,16,256]{3,2,1,0:T(8,128)}, f32[2,4,4,4,8,256]{5,4,3,2,1,0:T(8,128)}) custom-call(f32[4,12,16,256]{3,2,1,0:T(8,128)} %get-tuple-element.6.a, f32[2,4,4,4,8,256]{5,4,3,2,1,0:T(8,128)} %get-tuple-element.7.b), custom_call_target="tpu_custom_call" | custom-call | tf_op jit(solution)/shard_map/results/pallas_call | solution.py:670
  (4 shorter events, 0.0 us)

commit v4 on v3

--- a/solution.py
+++ b/solution.py
@@ -12,8 +12,8 @@
 BF16 = jnp.bfloat16
 KEEP = 36
 FIRST = 24
-QR = 3
-STAGES = 4
+QR = 2
+STAGES = 3
 ROWS = 128
 LAGS = (1, 3, 5, 7)
 
@@ -57,7 +57,7 @@
 
 def main_kernel(
     tab, g_hbm, f_hbm, inv_hbm, given, pid, dout,
-    nd, inv, nc, gv, out, ghi, glo, stage, ng0, ng1, nhi, nlo, pb, rc, ra, rb, rp, rm, rz, outx, ndt, pt, dw, dsum, e1, e2,
+    nd, inv, nc, gv, out, ghi, glo, stage, ng0, ng1, nhi, nlo, pb, rc, ra, rb, rp, rm, rz, outx0, outx1, ndt, pt, dw, dsum, e1, e2,
     in_sem, g_sem, p1_s, p1_r, xp_s, xp_r, xm_s, xm_r, z_s, z_r, c_s, c_r, rs_s, rs_r, ar_s, ar_r,
 ):
     x, y, zh, zl, c = coords()
@@ -93,7 +93,8 @@
     ins = (
         pltpu.make_async_copy(f_hbm, nd, in_sem.at[0]),
         pltpu.make_async_copy(inv_hbm, inv, in_sem.at[1]),
-        pltpu.make_async_copy(given.at[c, at[0], at[1], at[2]], gv, in_sem.at[2]),
+        pltpu.make_async_copy(given.at[c, at[0] % 2, at[1], at[2]], gv.at[0], in_sem.at[2]),
+        pltpu.make_async_copy(given.at[2 + c, at[0] % 2, at[1], at[2]], gv.at[1], in_sem.at[3]),
     )
     for cp in ins:
         cp.start()
@@ -162,8 +163,8 @@
             nc.at[pl.ds(base[h] + lo, hi - lo)], ng[h].at[pl.ds(lo, hi - lo), s_o], p1_r.at[h, i]
         )
 
-    def m_rows():
-        return rcopy(nd.at[pl.ds(2 * (1 - c), 2)], ndt, ar_s.at[0, 0], ar_r.at[0, 0], d_c)
+    def m_rows(w):
+        return rcopy(nd.at[2 * w + 1 - c], ndt.at[w], ar_s.at[w, 0], ar_r.at[w, 0], d_c)
 
     @pl.when(jnp.logical_not(own_target))
     def _():
@@ -357,9 +358,12 @@
         qs = pl.ds(g * QR, QR)
         return rcopy(pb.at[qs, y, 1 - zh, c], rz.at[qs], rs_s.at[5, g], rs_r.at[5, g], d_z2)
 
-    def m_out(g):
+    ready = FIRST // QR
+
+    def m_out(g, late):
         qs = pl.ds(g * QR, QR)
-        return rcopy(out.at[qs], outx.at[qs], rs_s.at[6, g], rs_r.at[6, g], d_c)
+        dst = outx1.at[pl.ds(g * QR - FIRST, QR)] if late else outx0.at[qs]
+        return rcopy(out.at[qs], dst, rs_s.at[6, g], rs_r.at[6, g], d_c)
 
 
     def m_down(n, w):
@@ -387,68 +391,79 @@
         part = dsum.at[w, c, (at[0] + 4 - n) % 4]
         return rcopy(part, part, ar_s.at[w, 37 + n], ar_r.at[w, 37 + n], d_c)
 
-    def diagonal():
-        for p in range(4):
+    def term(a, b):
+        return lax.dot_general(
+            a.reshape(192, 256), b.reshape(192, 256), (((0,), (0,)), ((), ())),
+            precision=lax.Precision.HIGHEST, preferred_element_type=F32,
+        )
+
+    def diag_steps(w):
+        def terms():
+            @pl.loop(ready if w else 0, rounds if w else ready)
+            def _(g):
+                m_out(g, w).wait_recv()
+
+            m_rows(w).wait_recv()
+            for p in (2 * w, 2 * w + 1):
+                for s in range(12):
+                    v = tab[3, p * 12 + s]
+                    pid[p, s] = jnp.where(v >= 0, out[jnp.maximum(v, 0)], 0.0)
+            p = 2 * w + c
             for s in range(12):
-                w = tab[3, p * 12 + s]
-                pid[p, s] = jnp.where(w >= 0, out[jnp.maximum(w, 0)], 0.0)
-        m_rows().wait_recv()
-
-        @pl.loop(0, rounds)
-        def _(g):
-            m_out(g).wait_recv()
-
-        def term(a, b):
-            return lax.dot_general(
-                a.reshape(192, 256), b.reshape(192, 256), (((0,), (0,)), ((), ())),
-                precision=lax.Precision.HIGHEST, preferred_element_type=F32,
-            )
-
-        for k in range(2):
-            p = 2 * c + k
-            for s in range(12):
-                w = tab[3, p * 12 + s]
-                pt[s] = jnp.where(w >= 0, outx[jnp.maximum(w, 0)], 0.0)
-            d = term(nd[p], pid[p]) + term(ndt[k], pt[...])
-            for w in (0, 1):
-                dw[w, 2 * k : 2 * k + 2] = d[:, 128 * w : 128 * w + 128].reshape(2, 4, 4, 8, 128)
-        both = (0, 1)
-        for w in both:
+                v = tab[3, p * 12 + s]
+                row = outx0[jnp.clip(v, 0, FIRST - 1)]
+                if w:
+                    more = outx1[jnp.clip(v - FIRST, 0, KEEP - FIRST - 1)]
+                    row = jnp.where(v >= FIRST, more, row)
+                pt[s] = jnp.where(v >= 0, row, 0.0)
+            d = term(nd[p], pid[p]) + term(ndt[w], pt[...])
+            dw[w, 0:2] = d[:, :128].reshape(2, 4, 4, 8, 128)
+            dw[w, 2:4] = d[:, 128:].reshape(2, 4, 4, 8, 128)
             for n in (1, 3, 2):
                 m_down(n, w).start()
-        for w in both:
+
+        def after_down():
             for n in (1, 3, 2):
                 m_down(n, w).wait_recv()
             dw[w, at[0]] = dw[w, at[0]] + (e1[w, 0] + e1[w, 1] + e1[w, 2])
             for n in plane:
                 m_plane(*n, w).start()
-        for w in both:
+
+        def after_plane():
             for n in plane:
                 m_plane(*n, w).wait_recv()
             total = dw[w, at[0], at[1], at[2]]
             for k in range(15):
                 total = total + e2[w, k]
-            dsum[w, c, at[0], at[1], at[2]] = gv[:, 128 * w : 128 * w + 128] - total
+            mine = jnp.where(at[0] < 2, gv[w, :, :128], gv[w, :, 128:])
+            dsum[w, c, at[0], at[1], at[2]] = mine - total
             for n in plane:
                 m_plane_up(*n, w).start()
-        for w in both:
+
+        def after_plane_up():
             for n in plane:
                 m_plane_up(*n, w).wait_recv()
             for n in (1, 3, 2):
                 m_up(n, w).start()
             m_twin(0, w).start()
-        for w in both:
+
+        def after_up():
             for n in (1, 3, 2):
                 m_up(n, w).wait_recv()
                 m_twin(n, w).start()
-        for w in both:
+
+        def done():
             for n in range(4):
                 m_twin(n, w).wait_recv()
-            dout[:, :, :, :, :, 128 * w : 128 * w + 128] = dsum[w]
+            for cc in (0, 1):
+                dout[2 * w + cc, :, :, :, :, 0:128] = dsum[w, cc, 0:2]
+                dout[2 * w + cc, :, :, :, :, 128:256] = dsum[w, cc, 2:4]
+
+        return terms, after_down, after_plane, after_plane_up, after_up, done
 
     def diagonal_sent():
-        m_rows().wait_send()
         for w in (0, 1):
+            m_rows(w).wait_send()
             for n in (1, 2, 3):
                 m_down(n, w).wait_send()
                 m_up(n, w).wait_send()
@@ -460,7 +475,8 @@
 
 
     one, two = gather_steps(0), gather_steps(1)
-    m_rows().start()
+    for w in (0, 1):
+        m_rows(w).start()
     some_g(0, G_FIRST)
     one[0]()
     some_g(G_FIRST, G_FIRST + 2)
@@ -479,6 +495,11 @@
     for n, r in zip(range(2, 10), GATHER_AT):
         under.setdefault(r, []).append(two[n])
     under.setdefault(early, []).append(lambda: spread(1))
+    diag0, diag1 = diag_steps(0), diag_steps(1)
+    inside = DIAG_AT[: sum(r < LAGS[3] + rounds for r in DIAG_AT)]
+    under_late = {}
+    for n, r in enumerate(inside):
+        under_late.setdefault(r, []).append(diag0[n])
 
     def step(i, carry):
         for r, acts in under.items():
@@ -547,12 +568,29 @@
                 q = g * QR + n
                 out[q] = -(pb[q, y, zh, c] + rz[q])
 
-            m_out(g).start()
+            @pl.when(g < ready)
+            def _():
+                m_out(g, False).start()
+
+            @pl.when(g >= ready)
+            def _():
+                m_out(g, True).start()
+
+        for r, acts in under_late.items():
+
+            @pl.when(i == r)
+            def _(acts=acts):
+                for act in acts:
+                    act()
 
         return carry
 
     lax.fori_loop(0, rounds + LAGS[3], step, 0)
-    diagonal()
+    rest = list(diag0[len(inside) :])
+    for act in diag1:
+        act()
+        if rest:
+            rest.pop(0)()
 
     @pl.when(jnp.logical_not(own_target))
     def _():
@@ -576,14 +614,33 @@
         m_p(g).wait_send()
         m_m(g).wait_send()
         m_z(g).wait_send()
-        m_out(g).wait_send()
+
+    @pl.loop(0, ready)
+    def _(g):
+        m_out(g, False).wait_send()
+
+    @pl.loop(ready, rounds)
+    def _(g):
+        m_out(g, True).wait_send()
 
     diagonal_sent()
 
 
-def results_kernel(a, b, a_out, b_out):
-    a_out[...] = a[...]
-    b_out[...] = b[...]
+def results_kernel(a, b, a_out, b_out, a_mid, b_mid, sem_in, sem_out):
+    parts = [
+        (src.at[p], mid.at[p], dst.at[p], 4 * n + p)
+        for p in range(4)
+        for n, (src, mid, dst) in enumerate(((a, a_mid, a_out), (b, b_mid, b_out)))
+    ]
+    first = [pltpu.make_async_copy(src, mid, sem_in.at[k]) for src, mid, _, k in parts]
+    second = [pltpu.make_async_copy(mid, dst, sem_out.at[k]) for _, mid, dst, k in parts]
+    for cp in first:
+        cp.start()
+    for came, goes in zip(first, second):
+        came.wait()
+        goes.start()
+    for cp in second:
+        cp.wait()
 
 
 VM = pl.BlockSpec(memory_space=pltpu.VMEM)
@@ -591,7 +648,8 @@
 ANY = pl.BlockSpec(memory_space=pl.ANY)
 DMA = pltpu.SemaphoreType.DMA
 G_FIRST = 10
-GATHER_AT = (1, 1, 2, 2, 3, 3, 4, 4)
+DIAG_AT = (20,)
+GATHER_AT = (1, 2, 3, 3, 4, 5, 5, 6)
 
 
 def on_device(
@@ -614,7 +672,7 @@
         main_kernel,
         out_shape=(
             jax.ShapeDtypeStruct((4, 12, 16, 256), F32),
-            jax.ShapeDtypeStruct((2, 4, 4, 4, 8, 256), F32),
+            jax.ShapeDtypeStruct((4, 2, 4, 4, 8, 256), F32),
         ),
         in_specs=[SM, ANY, ANY, ANY, ANY],
         out_specs=(VM, VM),
@@ -622,7 +680,7 @@
             pltpu.VMEM((4, 12, 16, 256), F32),
             pltpu.VMEM((4, 256, 256), F32),
             pltpu.VMEM((KEEP, 16, 256), F32),
-            pltpu.VMEM((8, 256), F32),
+            pltpu.VMEM((2, 8, 256), F32),
             pltpu.VMEM((KEEP, 16, 256), F32),
             pltpu.VMEM((12, 256, 1536), BF16),
             pltpu.VMEM((12, 256, 1536), BF16),
@@ -638,14 +696,15 @@
             pltpu.VMEM((KEEP, 2, 16, 256), F32),
             pltpu.VMEM((KEEP, 2, 16, 256), F32),
             pltpu.VMEM((KEEP, 16, 256), F32),
-            pltpu.VMEM((KEEP, 16, 256), F32),
+            pltpu.VMEM((FIRST, 16, 256), F32),
+            pltpu.VMEM((KEEP - FIRST, 16, 256), F32),
             pltpu.VMEM((2, 12, 16, 256), F32),
             pltpu.VMEM((12, 16, 256), F32),
             pltpu.VMEM((2, 4, 4, 4, 8, 128), F32),
             pltpu.VMEM((2, 2, 4, 4, 4, 8, 128), F32),
             pltpu.VMEM((2, 3, 4, 4, 8, 128), F32),
             pltpu.VMEM((2, 15, 8, 128), F32),
-            DMA((3,)),
+            DMA((4,)),
             DMA((STAGES,)),
             DMA((2, 2)),
             DMA((2, 2)),
@@ -666,12 +725,13 @@
             collective_id=0, has_side_effects=True, vmem_limit_bytes=67043328
         ),
         name="window",
-    )(tab, inverse_matrix, factor_blocks, factor_inverse, diag_given.reshape(2, 4, 4, 4, 8, 256))
+    )(tab, inverse_matrix, factor_blocks, factor_inverse, diag_given.reshape(4, 2, 4, 4, 8, 256))
     panel_inverse, diag = pl.pallas_call(
         results_kernel,
         out_shape=tuple(jax.ShapeDtypeStruct(v.shape, F32) for v in results),
-        in_specs=[VM, VM],
-        out_specs=(VM, VM),
+        in_specs=[ANY, ANY],
+        out_specs=(ANY, ANY),
+        scratch_shapes=[pltpu.VMEM(v.shape, F32) for v in results] + [DMA((8,)), DMA((8,))],
         name="results",
     )(*results)
     return (panel_inverse, diag.reshape(4, 256, 256))

time: 145 us -> 142 us (0.979)
  Pallas kernels: 140 us -> 138 us
    pallas_call x1, Pallas kernels: 137 us -> 135 us  [on_device(): pl.pallas_call(main_kernel, out_shape=(jax.ShapeDtypeStruct((4, 12, 16, 2...]
where the time goes in v4:
time: 142 us
  Pallas kernels  138 us (97%)
  other arithmetic  2.91 us (2%)
    pallas_call x1, Pallas kernels, on_device(): pl.pallas_call(main_kernel, out_shape=(jax.ShapeDtypeStruct((4, 12, 16, 2...  135 us

profile of v4, /device:TPU:1, one launch (start us, length us, event | category | flops | bytes accessed | tf_op | source)
XLA Modules:
  0.0 141.9 jit_solution(13295951654460386038)
XLA Ops:
  0.7 0.9 select_reduce_fusion.1
  1.6 0.9 select_reduce_fusion
  2.5 0.1 constant_dynamic-slice_fusion
  2.5 0.1 mul.74
  2.6 0.1 select_reduce_fusion.2
  2.7 0.1 reduce_sum.54
  2.8 0.1 compare_select_fusion
  2.9 0.1 constant_dynamic-slice_fusion.1
  3.0 0.1 reshape.43
  3.1 0.1 broadcast_compare_fusion
  3.1 0.1 gt.19
  3.2 0.1 mul.66
  3.3 0.1 select_reduce_fusion.3
  3.4 0.1 multiply_reduce_fusion
  3.6 0.6 pad_add_fusion.tab
  4.2 135.3 %window.1 = (f32[4,12,16,256]{3,2,1,0:T(8,128)}, f32[4,2,4,4,8,256]{5,4,3,2,1,0:T(8,128)}) custom-call(s32[4,48]{1,0:T(4,128)} %pad_add_fusion.tab, f32[3072,1536]{1,0:T(8,128)} %g_hbm.1, f32[4,12,16,256]{3,2,1,0:T(8,128)} %f_hbm.1, f32[4,256,256]{2,1,0:T(8,128)} %inv_hbm.1, f32[4,2,4,4,8,256]{5,4,3,2,1,0:T(8,128)} %bitcast.10), custom_call_target="tpu_custom_call" | custom-call | tf_op jit(solution)/shard_map/window/pallas_call | solution.py:671
  139.5 2.4 %results.1 = (f32[4,12,16,256]{3,2,1,0:T(8,128)}, f32[4,2,4,4,8,256]{5,4,3,2,1,0:T(8,128)}) custom-call(f32[4,12,16,256]{3,2,1,0:T(8,128)} %get-tuple-element.6.a, f32[4,2,4,4,8,256]{5,4,3,2,1,0:T(8,128)} %get-tuple-element.7.b), custom_call_target="tpu_custom_call" | custom-call | tf_op jit(solution)/shard_map/results/pallas_call | solution.py:729
  (4 shorter events, 0.0 us)

commit v5 on v4

--- a/solution.py
+++ b/solution.py
@@ -32,6 +32,14 @@
     hi = v.astype(BF16)
     lo = (v - hi.astype(F32)).astype(BF16)
     return hi, lo
+
+
+def dot3(a, b, dim):
+    (ah, al), (bh, bl) = split2(a), split2(b)
+    dims = (((dim,), (0,)), ((), ()))
+    out = lax.dot_general(ah, bh, dims, preferred_element_type=F32)
+    out += lax.dot_general(ah, bl, dims, preferred_element_type=F32)
+    return out + lax.dot_general(al, bh, dims, preferred_element_type=F32)
 
 
 def valid_slots(block_lists, list_mask, slot_of_block):
@@ -113,12 +121,7 @@
     for cp in ins:
         cp.wait()
     for p in range(4):
-        nd[p] = jnp.dot(
-            nd[p].reshape(192, 256),
-            inv[p],
-            precision=lax.Precision.HIGHEST,
-            preferred_element_type=F32,
-        ).reshape(12, 16, 256)
+        nd[p] = dot3(nd[p].reshape(192, 256), inv[p], 1).reshape(12, 16, 256)
 
     @pl.loop(0, KEEP)
     def _(q):
@@ -392,10 +395,7 @@
         return rcopy(part, part, ar_s.at[w, 37 + n], ar_r.at[w, 37 + n], d_c)
 
     def term(a, b):
-        return lax.dot_general(
-            a.reshape(192, 256), b.reshape(192, 256), (((0,), (0,)), ((), ())),
-            precision=lax.Precision.HIGHEST, preferred_element_type=F32,
-        )
+        return dot3(a.reshape(192, 256), b.reshape(192, 256), 0)
 
     def diag_steps(w):
         def terms():

time: 142 us -> 142 us (level)
  no operation moved by 1% of the time
where the time goes in v5:
time: 142 us
  Pallas kernels  138 us (97%)
  other arithmetic  2.91 us (2%)
    pallas_call x1, Pallas kernels, on_device(): pl.pallas_call(main_kernel, out_shape=(jax.ShapeDtypeStruct((4, 12, 16, 2...  135 us

profile of v5, /device:TPU:1, one launch (start us, length us, event | category | flops | bytes accessed | tf_op | source)
XLA Modules:
  0.0 141.9 jit_solution(4741105283965020927)
XLA Ops:
  0.7 0.9 select_reduce_fusion.1
  1.6 0.9 select_reduce_fusion
  2.5 0.1 constant_dynamic-slice_fusion
  2.5 0.1 mul.74
  2.6 0.1 select_reduce_fusion.2
  2.7 0.1 reduce_sum.54
  2.8 0.1 compare_select_fusion
  2.9 0.1 constant_dynamic-slice_fusion.1
  3.0 0.1 reshape.43
  3.1 0.1 broadcast_compare_fusion
  3.1 0.1 gt.19
  3.2 0.1 mul.66
  3.3 0.1 select_reduce_fusion.3
  3.4 0.1 multiply_reduce_fusion
  3.6 0.6 pad_add_fusion.tab
  4.2 135.3 %window.1 = (f32[4,12,16,256]{3,2,1,0:T(8,128)}, f32[4,2,4,4,8,256]{5,4,3,2,1,0:T(8,128)}) custom-call(s32[4,48]{1,0:T(4,128)} %pad_add_fusion.tab, f32[3072,1536]{1,0:T(8,128)} %g_hbm.1, f32[4,12,16,256]{3,2,1,0:T(8,128)} %f_hbm.1, f32[4,256,256]{2,1,0:T(8,128)} %inv_hbm.1, f32[4,2,4,4,8,256]{5,4,3,2,1,0:T(8,128)} %bitcast.10), custom_call_target="tpu_custom_call" | custom-call | tf_op jit(solution)/shard_map/window/pallas_call | solution.py:671
  139.5 2.4 %results.1 = (f32[4,12,16,256]{3,2,1,0:T(8,128)}, f32[4,2,4,4,8,256]{5,4,3,2,1,0:T(8,128)}) custom-call(f32[4,12,16,256]{3,2,1,0:T(8,128)} %get-tuple-element.6.a, f32[4,2,4,4,8,256]{5,4,3,2,1,0:T(8,128)} %get-tuple-element.7.b), custom_call_target="tpu_custom_call" | custom-call | tf_op jit(solution)/shard_map/results/pallas_call | solution.py:729
  (4 shorter events, 0.0 us)
